TPU v7x, 128 devices: a whole 4x4x4 slice. The times are simulated.
128 devices in a mesh: expert: 8 (over y, z_hi), dp: 16 (over x, z_lo, core).
Axes of the slice: x: 4, y: 4, z: 4 (z_hi: 2, z_lo: 2; z = z_hi * 2 + z_lo), core: 2. Of those that a mesh axis runs over, the one named last changes fastest.
Arguments:
- token_hidden: bfloat16 [16384, 2, 768], P(('expert', 'dp')), may hold values from -6 to 6
- token_grad: bfloat16 [16384, 2048], P(('expert', 'dp')), may hold values from -6 to 6
- routes: int32 [16384, 2], P(('expert', 'dp')), may hold values from 0 to 7, all different within a row; in each aligned block of 128 rows (0 to 127, 128 to 255, ...) at most 48 rows name the same one
- route_weight: float32 [16384, 2], P(('expert', 'dp')), may hold values from 0.2 to 1
- gradient_eigenbasis: bfloat16 [8, 2048, 2048], P('expert'), may hold values from -0.125 to 0.125
- basis_hidden: bfloat16 [8, 768, 768], P('expert'), may hold values from -0.21875 to 0.21875
- query_hidden: bfloat16 [8, 128, 768], P('expert', 'dp'), may hold values from -6 to 6
- query_grad: bfloat16 [8, 128, 2048], P('expert', 'dp'), may hold values from -6 to 6
- query_ids: int32 [8, 16], P('expert', 'dp'), may hold values from 0 to 7
- damping: float32 [8], P('expert'), may hold values from 0.05 to 0.5
Outputs:
- scores: float32 [16384, 2, 16], P(('expert', 'dp'))
- corrections: float32 [8, 2048, 768], P('expert', 'dp')
Inputs may be any that keep to these rules, and one draw needn't show every extreme that they name: `routes`: in each device's block of 128 tokens no expert is named by more than 48 rows, and a token's 2 experts differ. `query_ids`: each id names a row of the same device's block of 8 query examples of that expert.
All inputs are finite; a program needn't handle non-finite values.
Results may differ from a plain program's by a relative error of at most 0.0052.
Values may be sent and summed in bfloat16 or wider, within the bound.
A program may use at most 64 MiB of HBM per device.

v0:
```python
import math

import jax
import jax.numpy as jnp
from jax import lax
from jax.sharding import Mesh
from jax.sharding import PartitionSpec as P

DP = ("dp_0", "dp_1", "dp_2")
EXPERT_DP = ("expert", "dp_0", "dp_1", "dp_2")


eps = 1e-06


def split_up(shard, dim, peers):
    shape = shard.shape
    blocks = shard.reshape(*shape[:dim], peers, shape[dim] // peers, *shape[dim + 1 :])
    return jnp.moveaxis(blocks, dim, 0)


def summed_on_arrival(shard, axis, dim):
    peers = lax.axis_size(axis)
    blocks = lax.all_to_all(split_up(shard, dim, peers), axis, 0, 0, tiled=True)
    return jnp.sum(blocks, axis=0)


def sum_by_axis(shard, axes, dim):
    far, near = axes
    blocks = split_up(shard, dim, lax.axis_size(far))
    nearer = summed_on_arrival(blocks, near, dim + 1)
    arrived = lax.all_to_all(nearer, far, split_axis=0, concat_axis=0, tiled=True)
    return arrived.sum(axis=0)


def copy_for_each(shard, axis):
    copies = jnp.broadcast_to(shard, (lax.axis_size(axis), *shard.shape))
    return lax.all_to_all(copies, axis, split_axis=0, concat_axis=0, tiled=True)


def taken_together(shard, axis):
    everything = copy_for_each(shard, axis)
    return jnp.sum(everything, axis=0)


def laid_out(blocks, dim):
    shape = list(blocks.shape[1:])
    shape[dim] *= blocks.shape[0]
    return jnp.moveaxis(blocks, 0, dim).reshape(shape)


def gathered_by_axis(shard, axes, dim):
    far, near = axes
    blocks = copy_for_each(copy_for_each(shard, far), near)
    return laid_out(blocks.swapaxes(0, 1).reshape(-1, *shard.shape), dim)


def in_one_piece(arrays, axis, dim, along):
    widths = [a.shape[along] for a in arrays]
    both = jnp.concatenate(arrays, axis=along)
    out = lax.all_gather(both, axis, axis=dim, tiled=True)
    return tuple(jnp.split(out, [sum(widths[:k]) for k in range(1, len(widths))], axis=along))


def slot_index(routes_flat, experts, capacity):
    onehot = (routes_flat[:, None] == jnp.arange(experts, dtype=jnp.int32)[None, :]).astype(
        jnp.int32
    )
    before = jnp.cumsum(onehot, axis=0) - onehot
    return routes_flat * capacity + jnp.sum(before * onehot, axis=1)


def body(
    token_hidden,
    token_grad,
    routes,
    route_weight,
    gradient_eigenbasis,
    basis_hidden,
    query_hidden,
    query_grad,
    query_ids,
    damping,
):
    experts = lax.axis_size("expert")
    replicas = lax.axis_size(DP)
    tok_rows, top, width_ff = token_hidden.shape
    width_d = token_grad.shape[1]
    capacity = tok_rows * top * 3 // (2 * experts)
    slots = slot_index(routes.reshape(-1), experts, capacity)
    weighted = (route_weight[:, :, None] * token_grad[:, None, :].astype(jnp.float32)).astype(
        jnp.bfloat16
    )
    send_hidden = (
        jnp.zeros((experts * capacity, width_ff), jnp.bfloat16)
        .at[slots]
        .set(token_hidden.reshape(-1, width_ff))
        .reshape(experts, capacity, width_ff)
    )
    send_grad = (
        jnp.zeros((experts * capacity, width_d), jnp.bfloat16)
        .at[slots]
        .set(weighted.reshape(-1, width_d))
        .reshape(experts, capacity, width_d)
    )
    rotate_h = basis_hidden[0]
    rotate_gradient = gradient_eigenbasis[0]
    hidden = lax.all_to_all(send_hidden, "expert", split_axis=0, concat_axis=0, tiled=True)
    output_gradient = lax.all_to_all(send_grad, "expert", split_axis=0, concat_axis=0, tiled=True)
    hid = jnp.einsum("snf,fg->sng", hidden, rotate_h, preferred_element_type=jnp.float32).astype(
        jnp.bfloat16
    )
    gradient_rows = jnp.einsum(
        "zgc,cv->zgv", output_gradient, rotate_gradient, preferred_element_type=jnp.float32
    ).astype(jnp.bfloat16)
    hidden_flattened = hid.reshape(-1, width_ff)
    grad_flat = gradient_rows.reshape(-1, width_d)
    grad_sq = jnp.square(grad_flat.astype(jnp.float32)).astype(jnp.bfloat16)
    hid_sq = jnp.square(hidden_flattened.astype(jnp.float32)).astype(jnp.bfloat16)
    partial_score_value = jnp.einsum(
        "sd,sf->df", grad_sq, hid_sq, preferred_element_type=jnp.float32
    )
    scale = 1.0 / (replicas * experts * capacity)
    damp = damping[0]
    corrections = sum_by_axis(partial_score_value, (("dp_0", "dp_1"), "dp_2"), 0) * scale
    complete_sum = taken_together(jnp.sum(corrections), DP)
    level = damp * (complete_sum / (width_d * width_ff) + eps)
    inverse_portion = (1.0 / (corrections + level)).astype(jnp.bfloat16)
    inverse = gathered_by_axis(inverse_portion, (("dp_0", "dp_1"), "dp_2"), 0)
    picks = query_ids[0]
    query_g = jnp.take(query_grad[0], picks, axis=0)
    query_h = jnp.take(query_hidden[0], picks, axis=0)
    query_g_rot = jnp.dot(query_g, rotate_gradient, preferred_element_type=jnp.float32).astype(
        jnp.bfloat16
    )
    query_h_rot = jnp.dot(query_h, rotate_h, preferred_element_type=jnp.float32).astype(
        jnp.bfloat16
    )
    all_grad, all_hid = in_one_piece((query_g_rot, query_h_rot), DP, 0, 1)
    hid_wide = hidden_flattened.astype(jnp.float32)
    inverse_wide = inverse.astype(jnp.float32)
    root = math.sqrt(width_d * width_ff)

    def score_one(carry, pair):
        one_grad, one_hid = pair
        mixing = (
            inverse_wide
            * one_grad.astype(jnp.float32)[:, None]
            * one_hid.astype(jnp.float32)[None, :]
        ).astype(jnp.bfloat16)
        product = jnp.dot(grad_flat, mixing, preferred_element_type=jnp.float32)
        return (carry, jnp.sum(product * hid_wide, axis=1) / root)

    carry, slot_scores = lax.scan(score_one, jnp.zeros((), jnp.float32), (all_grad, all_hid))
    queries = all_grad.shape[0]
    returned = lax.all_to_all(
        slot_scores.T.reshape(experts, capacity, queries),
        "expert",
        split_axis=0,
        concat_axis=0,
        tiled=True,
    )
    scores = jnp.take(returned.reshape(-1, queries), slots, axis=0).reshape(tok_rows, top, queries)
    return (scores, corrections[None])


def solution(mesh):
    torus = Mesh(
        mesh.devices.reshape(mesh.shape["expert"], 4, 2, 2), ("expert", "dp_0", "dp_1", "dp_2")
    )
    placed = (
        P(EXPERT_DP, None, None),
        P(EXPERT_DP, None),
        P(EXPERT_DP, None),
        P(EXPERT_DP, None),
        P("expert", None, None),
        P("expert", None, None),
        P("expert", DP, None),
        P("expert", DP, None),
        P("expert", DP),
        P("expert"),
    )
    return jax.shard_map(
        body,
        mesh=torus,
        in_specs=placed,
        out_specs=(P(EXPERT_DP, None, None), P("expert", DP, None)),
        check_vma=False,
    )
```

profile of v0, /device:TPU:0, one launch (start us, length us, event | category | flops | bytes accessed | tf_op | source)
XLA Modules:
  0.0 289.8 jit_solution(8582748204176981344)
XLA Ops:
  0.6 0.9 copy.72
  1.8 0.7 broadcast_multiply_fusion.1
  2.5 0.6 reduce-window.6
  3.1 0.2 slice_reduce_fusion
  3.4 0.1 mul.86
  3.6 1.1 reshape.255
  4.8 2.5 scatter_custom_fusion.1
  7.3 7.9 %all-to-all-start.1 = ((bf16[8,48,768]{2,1,0:T(8,128)(2,1)}), bf16[8,48,768]{2,1,0:T(8,128)(2,1)}, u32[]{:S(2)}, u32[]{:S(2)}) async-start(bf16[8,48,768]{2,1,0:T(8,128)(2,1)} %bitcast.18), calls=%async_computation.1 | async-start | bytes 1179648 | tf_op jit(solution)/shard_map/all_to_all | solution.py:108
  15.2 2.1 mul.89
  17.3 2.5 mul.90
  20.1 4.5 %scatter_custom_fusion = bf16[384,2048]{1,0:T(8,128)(2,1)} fusion(s32[256]{0:T(256)S(1)} %bitcast.111, f32[256,2048]{1,0:T(8,128)} %mul.90, f32[256]{0:T(256)S(1)} %mul.87, bf16[]{:T(256)} %constant.80.clone.1), kind=kCustom, calls=%fused_computation.30 | custom fusion | flops 1048576 | bytes 3671042 | tf_op jit(solution)/shard_map/scatter | solution.py:103
  24.6 2.2 all-to-all-done.1
  26.8 5.0 %all-to-all-start = ((bf16[8,48,2048]{2,1,0:T(8,128)(2,1)}), bf16[8,48,2048]{2,1,0:T(8,128)(2,1)S(1)}, u32[]{:S(2)}, u32[]{:S(2)}) async-start(bf16[8,48,2048]{2,1,0:T(8,128)(2,1)} %bitcast.13), calls=%async_computation | async-start | bytes 3145728 | tf_op jit(solution)/shard_map/all_to_all | solution.py:109
  31.8 2.7 multiply_convert_fusion.10
  34.5 20.1 %all-to-all-done = bf16[8,48,2048]{2,1,0:T(8,128)(2,1)S(1)} async-done(((bf16[8,48,2048]{2,1,0:T(8,128)(2,1)}), bf16[8,48,2048]{2,1,0:T(8,128)(2,1)S(1)}, u32[]{:S(2)}, u32[]{:S(2)}) %all-to-all-start) | async-done | bytes 1572896 | tf_op jit(solution)/shard_map/all_to_all | solution.py:109
  54.6 6.8 %fusion.10 = bf16[8,48,2048]{2,1,0:T(8,128)(2,1)S(1)} fusion(bf16[8,48,2048]{2,1,0:T(8,128)(2,1)S(1)} %all-to-all-done, bf16[1,2048,2048]{2,1,0:T(8,128)(2,1)} %param.16), kind=kOutput, calls=%fused_computation.19 | convolution fusion | flops 3222011904 | bytes 11534336 | tf_op jit(solution)/shard_map/zgc,cv->zgv/dot_general | solution.py:113
  61.4 1.2 copy-done.2
  62.6 1.6 fusion.13
  64.2 1.9 copy.86
  66.1 1.8 convolution_bitcast_fusion
  67.9 0.6 copy.78
  68.5 10.0 %all_to_all.41 = f32[2,8,128,768]{3,2,1,0:T(8,128)} all-to-all(f32[2,8,128,768]{3,2,1,0:T(8,128)S(1)} %copy.78), channel_id=1, replica_groups=mesh['expert'=8,'dp_0'=4,'dp_1'=2,'dp_2'=2] {'dp_2'}, dimensions={0} | all-to-all | bytes 12582912 | tf_op jit(solution)/shard_map/all_to_all | solution.py:24
  78.5 5.3 %reduce_sum.61 = f32[8,128,768]{2,1,0:T(8,128)} reduce(f32[2,8,128,768]{3,2,1,0:T(8,128)} %all_to_all.41, f32[]{:T(128)} %constant.55.clone.1), dimensions={0}, to_apply=%region_5.6 | reduce | flops 786432 | bytes 9437188 | tf_op jit(solution)/shard_map/reduce_sum | solution.py:25
  83.8 43.0 %all_to_all.42 = f32[8,128,768]{2,1,0:T(8,128)} all-to-all(f32[8,128,768]{2,1,0:T(8,128)} %reduce_sum.61), channel_id=1, replica_groups=mesh['expert'=8,'dp_0'=4,'dp_1'=2,'dp_2'=2] {'dp_0','dp_1'}, dimensions={0} | all-to-all | bytes 6291456 | tf_op jit(solution)/shard_map/all_to_all | solution.py:32
  126.7 2.1 reduce_sum.62
  128.8 0.7 multiply_reduce_fusion
  129.5 1.2 broadcast_in_dim.69
  130.8 3.5 %all-to-all-start.4 = ((f32[16,1,1]{2,1,0:T(1,128)}), f32[16,1,1]{2,1,0:T(1,128)S(1)}, u32[]{:S(2)}, u32[]{:S(2)}) async-start(f32[16,1,1]{2,1,0:T(1,128)} %broadcast_in_dim.69), calls=%async_computation.4 | async-start | bytes 16384 | tf_op jit(solution)/shard_map/all_to_all | solution.py:38
  134.9 5.3 %all-to-all-done.4 = f32[16,1,1]{2,1,0:T(1,128)S(1)} async-done(((f32[16,1,1]{2,1,0:T(1,128)}), f32[16,1,1]{2,1,0:T(1,128)S(1)}, u32[]{:S(2)}, u32[]{:S(2)}) %all-to-all-start.4) | async-done | bytes 96 | tf_op jit(solution)/shard_map/all_to_all | solution.py:38
  140.2 0.6 reduce_sum.64
  141.5 0.8 multiply_bitcast_fusion
  142.3 1.3 broadcast_in_dim.70
  143.5 3.6 %all-to-all-start.5 = ((bf16[8,128,768]{2,1,0:T(8,128)(2,1)}), bf16[8,128,768]{2,1,0:T(8,128)(2,1)S(1)}, u32[]{:S(2)}, u32[]{:S(2)}) async-start(bf16[8,128,768]{2,1,0:T(8,128)(2,1)} %broadcast_in_dim.70), calls=%async_computation.5 | async-start | bytes 3145728 | tf_op jit(solution)/shard_map/all_to_all | solution.py:38
  147.8 4.6 %fusion.8 = f32[1,2048]{1,0:T(1,128)S(1)} fusion(bf16[1,2048,2048]{2,1,0:T(8,128)(2,1)} %param.16, pred[]{:T(512)} %bitcast.5, bf16[1,8,2048]{2,1,0:T(8,128)(2,1)} %param.19, s32[]{:T(128)} %bitcast.6), kind=kOutput, calls=%fused_computation.15 | convolution fusion | flops 8390656 | bytes 8406016 | tf_op jit(solution)/shard_map/dot_general | solution.py:133
  152.4 1.0 fusion.18
  153.5 27.0 %all-gather = bf16[16,1,2816]{2,1,0:T(2,128)(2,1)S(1)} all-gather(bf16[1,1,2816]{2,1,0:T(2,128)(2,1)S(1)} %maximum_bitcast_fusion), channel_id=1, replica_groups=mesh['expert'=8,'dp_0'=4,'dp_1'=2,'dp_2'=2] {'dp_0','dp_1','dp_2'}, dimensions={0}, use_global_device_ids=true | all-gather | bytes 95744 | tf_op jit(solution)/shard_map/all_gather | solution.py:61
  180.8 1.6 copy.81
  182.4 0.3 broadcast_in_dim.71
  182.8 6.3 %all_to_all.43 = bf16[2,8,128,768]{3,2,1,0:T(8,128)(2,1)S(1)} all-to-all(bf16[2,8,128,768]{3,2,1,0:T(8,128)(2,1)S(1)} %broadcast_in_dim.71), channel_id=1, replica_groups=mesh['expert'=8,'dp_0'=4,'dp_1'=2,'dp_2'=2] {'dp_2'}, dimensions={0} | all-to-all | bytes 6291456 | tf_op jit(solution)/shard_map/all_to_all | solution.py:38
  189.1 3.3 %copy_convert_fusion = f32[2,8,128,768]{3,2,0,1:T(8,128)} fusion(bf16[2,8,128,768]{3,2,1,0:T(8,128)(2,1)S(1)} %all_to_all.43), kind=kLoop, calls=%fused_computation.17 | loop fusion | flops 1572864 | bytes 9437184 | tf_op jit(solution)/shard_map/convert_element_type | solution.py:141
  192.4 82.7 %while.12 = (s32[]{:T(128)}, f32[16,384]{1,0:T(8,128)S(1)}, bf16[16,2048]{1,0:T(8,128)(2,1)S(1)}, f32[2048,768]{1,0:T(8,128)}, bf16[16,768]{1,0:T(8,128)(2,1)S(1...) while((s32[]{:T(128)}, f32[16,384]{1,0:T(8,128)S(1)}, ...), condition=%wide.region_11.12_spmd, body=%wide.region_9.11_spmd.sunk | while | flops 1213270784 | bytes 9082985 | solution.py:154
  192.5 5.0 %fusion.49 = f32[384]{0:T(512)S(1)} fusion(f32[384,768]{0,1:T(8,128)S(1)} %get-tuple-element.196, bf16[384,2048]{1,0:T(8,128)(2,1)S(1)} %get-tuple-element.195, f32[2048,768]{1,0:T(8,128)} %get-tuple-element.193, f32[768]{0:T(1024)S(1)} %convert_reduce_fusion.2, f32[2048]{0:T(1024)S(1)} %bitcast.106), kind=kOutput, calls=%fused_computation.9.clone.1 | convolution fusion | flops 1213267584 | bytes 9056768 | tf_op jit(solution)/shard_map/while/body/eval_jaxpr/dot_general | solution.py:151
  197.7 5.0 %fusion.49 = f32[384]{0:T(512)S(1)} fusion(f32[384,768]{0,1:T(8,128)S(1)} %get-tuple-element.196, bf16[384,2048]{1,0:T(8,128)(2,1)S(1)} %get-tuple-element.195, f32[2048,768]{1,0:T(8,128)} %get-tuple-element.193, f32[768]{0:T(1024)S(1)} %convert_reduce_fusion.2, f32[2048]{0:T(1024)S(1)} %bitcast.106), kind=kOutput, calls=%fused_computation.9.clone.1 | convolution fusion | flops 1213267584 | bytes 9056768 | tf_op jit(solution)/shard_map/while/body/eval_jaxpr/dot_general | solution.py:151
  202.8 5.0 %fusion.49 = f32[384]{0:T(512)S(1)} fusion(f32[384,768]{0,1:T(8,128)S(1)} %get-tuple-element.196, bf16[384,2048]{1,0:T(8,128)(2,1)S(1)} %get-tuple-element.195, f32[2048,768]{1,0:T(8,128)} %get-tuple-element.193, f32[768]{0:T(1024)S(1)} %convert_reduce_fusion.2, f32[2048]{0:T(1024)S(1)} %bitcast.106), kind=kOutput, calls=%fused_computation.9.clone.1 | convolution fusion | flops 1213267584 | bytes 9056768 | tf_op jit(solution)/shard_map/while/body/eval_jaxpr/dot_general | solution.py:151
  208.0 5.0 %fusion.49 = f32[384]{0:T(512)S(1)} fusion(f32[384,768]{0,1:T(8,128)S(1)} %get-tuple-element.196, bf16[384,2048]{1,0:T(8,128)(2,1)S(1)} %get-tuple-element.195, f32[2048,768]{1,0:T(8,128)} %get-tuple-element.193, f32[768]{0:T(1024)S(1)} %convert_reduce_fusion.2, f32[2048]{0:T(1024)S(1)} %bitcast.106), kind=kOutput, calls=%fused_computation.9.clone.1 | convolution fusion | flops 1213267584 | bytes 9056768 | tf_op jit(solution)/shard_map/while/body/eval_jaxpr/dot_general | solution.py:151
  213.2 5.0 %fusion.49 = f32[384]{0:T(512)S(1)} fusion(f32[384,768]{0,1:T(8,128)S(1)} %get-tuple-element.196, bf16[384,2048]{1,0:T(8,128)(2,1)S(1)} %get-tuple-element.195, f32[2048,768]{1,0:T(8,128)} %get-tuple-element.193, f32[768]{0:T(1024)S(1)} %convert_reduce_fusion.2, f32[2048]{0:T(1024)S(1)} %bitcast.106), kind=kOutput, calls=%fused_computation.9.clone.1 | convolution fusion | flops 1213267584 | bytes 9056768 | tf_op jit(solution)/shard_map/while/body/eval_jaxpr/dot_general | solution.py:151
  218.3 5.0 %fusion.49 = f32[384]{0:T(512)S(1)} fusion(f32[384,768]{0,1:T(8,128)S(1)} %get-tuple-element.196, bf16[384,2048]{1,0:T(8,128)(2,1)S(1)} %get-tuple-element.195, f32[2048,768]{1,0:T(8,128)} %get-tuple-element.193, f32[768]{0:T(1024)S(1)} %convert_reduce_fusion.2, f32[2048]{0:T(1024)S(1)} %bitcast.106), kind=kOutput, calls=%fused_computation.9.clone.1 | convolution fusion | flops 1213267584 | bytes 9056768 | tf_op jit(solution)/shard_map/while/body/eval_jaxpr/dot_general | solution.py:151
  223.5 5.0 %fusion.49 = f32[384]{0:T(512)S(1)} fusion(f32[384,768]{0,1:T(8,128)S(1)} %get-tuple-element.196, bf16[384,2048]{1,0:T(8,128)(2,1)S(1)} %get-tuple-element.195, f32[2048,768]{1,0:T(8,128)} %get-tuple-element.193, f32[768]{0:T(1024)S(1)} %convert_reduce_fusion.2, f32[2048]{0:T(1024)S(1)} %bitcast.106), kind=kOutput, calls=%fused_computation.9.clone.1 | convolution fusion | flops 1213267584 | bytes 9056768 | tf_op jit(solution)/shard_map/while/body/eval_jaxpr/dot_general | solution.py:151
  228.7 5.0 %fusion.49 = f32[384]{0:T(512)S(1)} fusion(f32[384,768]{0,1:T(8,128)S(1)} %get-tuple-element.196, bf16[384,2048]{1,0:T(8,128)(2,1)S(1)} %get-tuple-element.195, f32[2048,768]{1,0:T(8,128)} %get-tuple-element.193, f32[768]{0:T(1024)S(1)} %convert_reduce_fusion.2, f32[2048]{0:T(1024)S(1)} %bitcast.106), kind=kOutput, calls=%fused_computation.9.clone.1 | convolution fusion | flops 1213267584 | bytes 9056768 | tf_op jit(solution)/shard_map/while/body/eval_jaxpr/dot_general | solution.py:151
  233.9 5.0 %fusion.49 = f32[384]{0:T(512)S(1)} fusion(f32[384,768]{0,1:T(8,128)S(1)} %get-tuple-element.196, bf16[384,2048]{1,0:T(8,128)(2,1)S(1)} %get-tuple-element.195, f32[2048,768]{1,0:T(8,128)} %get-tuple-element.193, f32[768]{0:T(1024)S(1)} %convert_reduce_fusion.2, f32[2048]{0:T(1024)S(1)} %bitcast.106), kind=kOutput, calls=%fused_computation.9.clone.1 | convolution fusion | flops 1213267584 | bytes 9056768 | tf_op jit(solution)/shard_map/while/body/eval_jaxpr/dot_general | solution.py:151
  239.0 5.0 %fusion.49 = f32[384]{0:T(512)S(1)} fusion(f32[384,768]{0,1:T(8,128)S(1)} %get-tuple-element.196, bf16[384,2048]{1,0:T(8,128)(2,1)S(1)} %get-tuple-element.195, f32[2048,768]{1,0:T(8,128)} %get-tuple-element.193, f32[768]{0:T(1024)S(1)} %convert_reduce_fusion.2, f32[2048]{0:T(1024)S(1)} %bitcast.106), kind=kOutput, calls=%fused_computation.9.clone.1 | convolution fusion | flops 1213267584 | bytes 9056768 | tf_op jit(solution)/shard_map/while/body/eval_jaxpr/dot_general | solution.py:151
  244.2 5.0 %fusion.49 = f32[384]{0:T(512)S(1)} fusion(f32[384,768]{0,1:T(8,128)S(1)} %get-tuple-element.196, bf16[384,2048]{1,0:T(8,128)(2,1)S(1)} %get-tuple-element.195, f32[2048,768]{1,0:T(8,128)} %get-tuple-element.193, f32[768]{0:T(1024)S(1)} %convert_reduce_fusion.2, f32[2048]{0:T(1024)S(1)} %bitcast.106), kind=kOutput, calls=%fused_computation.9.clone.1 | convolution fusion | flops 1213267584 | bytes 9056768 | tf_op jit(solution)/shard_map/while/body/eval_jaxpr/dot_general | solution.py:151
  249.4 5.0 %fusion.49 = f32[384]{0:T(512)S(1)} fusion(f32[384,768]{0,1:T(8,128)S(1)} %get-tuple-element.196, bf16[384,2048]{1,0:T(8,128)(2,1)S(1)} %get-tuple-element.195, f32[2048,768]{1,0:T(8,128)} %get-tuple-element.193, f32[768]{0:T(1024)S(1)} %convert_reduce_fusion.2, f32[2048]{0:T(1024)S(1)} %bitcast.106), kind=kOutput, calls=%fused_computation.9.clone.1 | convolution fusion | flops 1213267584 | bytes 9056768 | tf_op jit(solution)/shard_map/while/body/eval_jaxpr/dot_general | solution.py:151
  254.5 5.0 %fusion.49 = f32[384]{0:T(512)S(1)} fusion(f32[384,768]{0,1:T(8,128)S(1)} %get-tuple-element.196, bf16[384,2048]{1,0:T(8,128)(2,1)S(1)} %get-tuple-element.195, f32[2048,768]{1,0:T(8,128)} %get-tuple-element.193, f32[768]{0:T(1024)S(1)} %convert_reduce_fusion.2, f32[2048]{0:T(1024)S(1)} %bitcast.106), kind=kOutput, calls=%fused_computation.9.clone.1 | convolution fusion | flops 1213267584 | bytes 9056768 | tf_op jit(solution)/shard_map/while/body/eval_jaxpr/dot_general | solution.py:151
  259.7 5.0 %fusion.49 = f32[384]{0:T(512)S(1)} fusion(f32[384,768]{0,1:T(8,128)S(1)} %get-tuple-element.196, bf16[384,2048]{1,0:T(8,128)(2,1)S(1)} %get-tuple-element.195, f32[2048,768]{1,0:T(8,128)} %get-tuple-element.193, f32[768]{0:T(1024)S(1)} %convert_reduce_fusion.2, f32[2048]{0:T(1024)S(1)} %bitcast.106), kind=kOutput, calls=%fused_computation.9.clone.1 | convolution fusion | flops 1213267584 | bytes 9056768 | tf_op jit(solution)/shard_map/while/body/eval_jaxpr/dot_general | solution.py:151
  264.9 5.0 %fusion.49 = f32[384]{0:T(512)S(1)} fusion(f32[384,768]{0,1:T(8,128)S(1)} %get-tuple-element.196, bf16[384,2048]{1,0:T(8,128)(2,1)S(1)} %get-tuple-element.195, f32[2048,768]{1,0:T(8,128)} %get-tuple-element.193, f32[768]{0:T(1024)S(1)} %convert_reduce_fusion.2, f32[2048]{0:T(1024)S(1)} %bitcast.106), kind=kOutput, calls=%fused_computation.9.clone.1 | convolution fusion | flops 1213267584 | bytes 9056768 | tf_op jit(solution)/shard_map/while/body/eval_jaxpr/dot_general | solution.py:151
  270.0 5.0 %fusion.49 = f32[384]{0:T(512)S(1)} fusion(f32[384,768]{0,1:T(8,128)S(1)} %get-tuple-element.196, bf16[384,2048]{1,0:T(8,128)(2,1)S(1)} %get-tuple-element.195, f32[2048,768]{1,0:T(8,128)} %get-tuple-element.193, f32[768]{0:T(1024)S(1)} %convert_reduce_fusion.2, f32[2048]{0:T(1024)S(1)} %bitcast.106), kind=kOutput, calls=%fused_computation.9.clone.1 | convolution fusion | flops 1213267584 | bytes 9056768 | tf_op jit(solution)/shard_map/while/body/eval_jaxpr/dot_general | solution.py:151
  275.3 0.7 reshape.277
  276.0 3.3 %all-to-all-start.7 = ((f32[8,1,768]{2,1,0:T(1,128)}), f32[8,1,768]{2,1,0:T(1,128)S(1)}, u32[]{:S(2)}, u32[]{:S(2)}) async-start(f32[8,1,768]{2,1,0:T(1,128)} %reshape.277), calls=%async_computation.7 | async-start | bytes 49152 | tf_op jit(solution)/shard_map/all_to_all | solution.py:156
  279.3 7.6 %all-to-all-done.7 = f32[8,1,768]{2,1,0:T(1,128)S(1)} async-done(((f32[8,1,768]{2,1,0:T(1,128)}), f32[8,1,768]{2,1,0:T(1,128)S(1)}, u32[]{:S(2)}, u32[]{:S(2)}) %all-to-all-start.7) | async-done | bytes 24608 | tf_op jit(solution)/shard_map/all_to_all | solution.py:156
  287.0 0.5 broadcast.213
  287.5 0.7 reduce.7
  288.4 0.7 gather_fusion
  289.2 0.6 broadcast_select_fusion.1
  (119 shorter events, 3.1 us)
Async XLA Ops:
  0.6 31.2 %copy-start = (bf16[1,768,768]{2,1,0:T(8,128)(2,1)S(1)}, bf16[1,768,768]{2,1,0:T(8,128)(2,1)}, u32[]{:S(2)}) copy-start(bf16[1,768,768]{2,1,0:T(8,128)(2,1)} %param.17) | copy-start | bytes 3538948
  7.3 19.5 %all-to-all-start.1 = ((bf16[8,48,768]{2,1,0:T(8,128)(2,1)}), bf16[8,48,768]{2,1,0:T(8,128)(2,1)}, u32[]{:S(2)}, u32[]{:S(2)}) async-start(bf16[8,48,768]{2,1,0:T(8,128)(2,1)} %bitcast.18), calls=%async_computation.1 | async-start | bytes 1179648 | tf_op jit(solution)/shard_map/all_to_all | solution.py:108
  17.3 2.5 copy-start.5
  26.8 27.8 %all-to-all-start = ((bf16[8,48,2048]{2,1,0:T(8,128)(2,1)}), bf16[8,48,2048]{2,1,0:T(8,128)(2,1)S(1)}, u32[]{:S(2)}, u32[]{:S(2)}) async-start(bf16[8,48,2048]{2,1,0:T(8,128)(2,1)} %bitcast.13), calls=%async_computation | async-start | bytes 3145728 | tf_op jit(solution)/shard_map/all_to_all | solution.py:109
  61.4 1.2 copy-start.2
  130.8 9.4 %all-to-all-start.4 = ((f32[16,1,1]{2,1,0:T(1,128)}), f32[16,1,1]{2,1,0:T(1,128)S(1)}, u32[]{:S(2)}, u32[]{:S(2)}) async-start(f32[16,1,1]{2,1,0:T(1,128)} %broadcast_in_dim.69), calls=%async_computation.4 | async-start | bytes 16384 | tf_op jit(solution)/shard_map/all_to_all | solution.py:38
  143.5 38.9 %all-to-all-start.5 = ((bf16[8,128,768]{2,1,0:T(8,128)(2,1)}), bf16[8,128,768]{2,1,0:T(8,128)(2,1)S(1)}, u32[]{:S(2)}, u32[]{:S(2)}) async-start(bf16[8,128,768]{2,1,0:T(8,128)(2,1)} %broadcast_in_dim.70), calls=%async_computation.5 | async-start | bytes 3145728 | tf_op jit(solution)/shard_map/all_to_all | solution.py:38
  152.4 28.4 %copy-start.4 = (s32[128,2]{0,1:T(2,128)S(1)}, s32[128,2]{0,1:T(2,128)}, u32[]{:S(2)}) copy-start(s32[128,2]{0,1:T(2,128)} %param.14) | copy-start | bytes 3076
  189.1 3.3 %copy-start.3 = (bf16[8,48,2048]{2,1,0:T(8,128)(2,1)S(1)}, bf16[8,48,2048]{2,1,0:T(8,128)(2,1)}, u32[]{:S(2)}) copy-start(bf16[8,48,2048]{2,1,0:T(8,128)(2,1)} %copy-done.2) | copy-start | bytes 4718596
  275.2 14.7 %copy-start.1 = (bf16[1,768,768]{2,1,0:T(8,128)(2,1)S(1)}, bf16[1,768,768]{2,1,0:T(8,128)(2,1)}, u32[]{:S(2)}) copy-start(bf16[1,768,768]{2,1,0:T(8,128)(2,1)} %param.17) | copy-start | bytes 3538948
  276.0 11.0 %all-to-all-start.7 = ((f32[8,1,768]{2,1,0:T(1,128)}), f32[8,1,768]{2,1,0:T(1,128)S(1)}, u32[]{:S(2)}, u32[]{:S(2)}) async-start(f32[8,1,768]{2,1,0:T(1,128)} %reshape.277), calls=%async_computation.7 | async-start | bytes 49152 | tf_op jit(solution)/shard_map/all_to_all | solution.py:156
where the time goes:
time: 291 us; the launch traced here: 290 us
  matrix products  97.3 us (33%)
  blocking collectives  86.3 us (30%)
  waiting for transfers between devices  35.2 us (12%)
  starting transfers between devices  23.3 us (8%)
  other arithmetic  22.5 us (8%)
  local copies, waits for them, and re-layouts  21.7 us (7%)
    dot_general x16, matrix products, score_one(): product = jnp.dot(grad_flat, mixing, preferred_element_type=jnp.float32)  80.4 us
    all_to_all x1, blocking collectives, sum_by_axis(): lax.all_to_all(nearer, far, split_axis=0, concat_axis=0, tiled=True)  43 us
    all_gather x1, blocking collectives, in_one_piece(): out = lax.all_gather(both, axis, axis=dim, tiled=True)  27 us
    all_to_all x1, waiting for transfers between devices, body(): lax.all_to_all(send_grad, 'expert', split_axis=0, concat_axis=0, tiled=True)  20.1 us
    all_to_all x1, blocking collectives, summed_on_arrival(): blocks = lax.all_to_all(split_up(shard, dim, peers), axis, 0, 0, tiled=True)  9.99 us
    all_to_all x1, starting transfers between devices, body(): lax.all_to_all(send_hidden, 'expert', split_axis=0, concat_axis=0, tiled=...  7.89 us
    all_to_all x1, waiting for transfers between devices, body(): lax.all_to_all(slot_scores.T.reshape(experts, capacity, queries), 'expert...  7.62 us
    all_to_all x2, starting transfers between devices, copy_for_each(): return lax.all_to_all(copies, axis, split_axis=0, concat_axis=0, tiled=True)  7.05 us
  transfers between devices with their start and end apart: 5, of which 4 were waited for; matrix products, arithmetic and copies ran while one was open for 7% of the time, Pallas kernels for 0%

commit v1 on v0

v1 whole, which is shorter than its diff:
```python
import functools
import math

import jax
import jax.numpy as jnp
from jax import lax
from jax.experimental import pallas as pl
from jax.experimental.pallas import tpu as pltpu
from jax.sharding import Mesh
from jax.sharding import PartitionSpec as P

DP = ("dp_0", "dp_1", "dp_2")
EXPERT_DP = ("expert", "dp_0", "dp_1", "dp_2")

eps = 1e-06


def score_kernel(group, g_ref, h_ref, inv_ref, qg_ref, qh_ref, out_ref):
    rows = g_ref.shape[0]
    lane = lax.broadcasted_iota(jnp.int32, out_ref.shape, 1)
    step = pl.program_id(0)
    gq = jnp.concatenate(
        [g_ref[...] * qg_ref[k].astype(jnp.bfloat16) for k in range(group)], axis=0
    )
    product = jnp.dot(gq, inv_ref[...], preferred_element_type=jnp.float32)
    wide = h_ref[...].astype(jnp.float32)

    @pl.when(step == 0)
    def _():
        out_ref[...] = jnp.zeros_like(out_ref)

    total = out_ref[...]
    for k in range(group):
        n = step * group + k
        value = jnp.sum(product[k * rows : (k + 1) * rows] * (wide * qh_ref[k]), axis=1, keepdims=True)
        total = jnp.where(lane == n, value, total)
    out_ref[...] = total


def scored(g, h, inverse, qg, qh, group=2):
    rows = g.shape[0]
    queries = qg.shape[0]
    whole = lambda a: pl.BlockSpec(a.shape, lambda n: (0, 0), pipeline_mode=pl.Buffered(1))
    out = pl.pallas_call(
        functools.partial(score_kernel, group),
        grid=(queries // group,),
        in_specs=[whole(a) for a in (g, h, inverse)]
        + [pl.BlockSpec((group, 1, a.shape[2]), lambda n: (n, 0, 0)) for a in (qg, qh)],
        out_specs=pl.BlockSpec((rows, 128), lambda n: (0, 0)),
        out_shape=jax.ShapeDtypeStruct((rows, 128), jnp.float32),
        compiler_params=pltpu.CompilerParams(vmem_limit_bytes=50 * 1024 * 1024),
    )(g, h, inverse, qg, qh)
    return out[:, :queries]


def slot_index(routes_flat, experts, capacity):
    onehot = (routes_flat[:, None] == jnp.arange(experts, dtype=jnp.int32)[None, :]).astype(
        jnp.int32
    )
    before = jnp.cumsum(onehot, axis=0) - onehot
    return routes_flat * capacity + jnp.sum(before * onehot, axis=1)


def traded(blocks, axis):
    return lax.all_to_all(blocks, axis, split_axis=0, concat_axis=0, tiled=True)


def for_each(shard, axis):
    return traded(jnp.broadcast_to(shard, (lax.axis_size(axis), *shard.shape)), axis)


def body(
    token_hidden,
    token_grad,
    routes,
    route_weight,
    gradient_eigenbasis,
    basis_hidden,
    query_hidden,
    query_grad,
    query_ids,
    damping,
):
    experts = lax.axis_size("expert")
    replicas = lax.axis_size(DP)
    tok_rows, top, width_ff = token_hidden.shape
    width_d = token_grad.shape[1]
    capacity = tok_rows * top * 3 // (2 * experts)
    slots = slot_index(routes.reshape(-1), experts, capacity)
    weighted = (route_weight[:, :, None] * token_grad[:, None, :].astype(jnp.float32)).astype(
        jnp.bfloat16
    )
    rows = jnp.concatenate(
        (token_hidden.reshape(-1, width_ff), weighted.reshape(-1, width_d)), axis=1
    )
    chosen = (slots[None, :] == jnp.arange(experts * capacity, dtype=jnp.int32)[:, None]).astype(
        jnp.bfloat16
    )
    sent = jnp.dot(chosen, rows, preferred_element_type=jnp.float32).astype(jnp.bfloat16)
    held = traded(sent.reshape(experts, capacity, -1), "expert").reshape(experts * capacity, -1)
    rotate_h = basis_hidden[0]
    rotate_gradient = gradient_eigenbasis[0]
    picks = query_ids[0]
    query_g = jnp.take(query_grad[0], picks, axis=0)
    query_h = jnp.take(query_hidden[0], picks, axis=0)
    query_g_rot = jnp.dot(query_g, rotate_gradient, preferred_element_type=jnp.float32)
    query_h_rot = jnp.dot(query_h, rotate_h, preferred_element_type=jnp.float32)
    hid = jnp.dot(held[:, :width_ff], rotate_h, preferred_element_type=jnp.float32).astype(
        jnp.bfloat16
    )
    grad = jnp.dot(held[:, width_ff:], rotate_gradient, preferred_element_type=jnp.float32).astype(
        jnp.bfloat16
    )
    grad_sq = jnp.square(grad.astype(jnp.float32)).astype(jnp.bfloat16)
    hid_sq = jnp.square(hid.astype(jnp.float32)).astype(jnp.bfloat16)
    own_sum = jnp.sum(
        jnp.sum(grad_sq.astype(jnp.float32), axis=1) * jnp.sum(hid_sq.astype(jnp.float32), axis=1)
    )
    partial = lax.dot_general(
        grad_sq, hid_sq, (((0,), (0,)), ((), ())), preferred_element_type=jnp.float32
    ).astype(jnp.bfloat16)
    scale = 1.0 / (replicas * experts * capacity)
    chips = lax.axis_size(("dp_0", "dp_1"))
    part = width_d // replicas
    blocks = partial.reshape(chips, 2, part, width_ff).swapaxes(0, 1)
    near = traded(blocks, "dp_2").astype(jnp.float32).sum(axis=0).astype(jnp.bfloat16)
    far = traded(near, ("dp_0", "dp_1"))
    corrections = far.astype(jnp.float32).sum(axis=0) * scale

    small = jnp.concatenate(
        (query_g_rot, query_h_rot, jnp.broadcast_to(own_sum, (query_g.shape[0], 128))), axis=1
    )
    small = for_each(small, DP)
    small = small.reshape(-1, 1, small.shape[-1])
    rounded = small[:, :, : width_d + width_ff].astype(jnp.bfloat16).astype(jnp.float32)
    all_grad = rounded[:, :, :width_d]
    all_hid = rounded[:, :, width_d:]
    complete = jnp.sum(small[:: small.shape[0] // replicas, 0, -1]) * scale
    level = damping[0] * (complete / (width_d * width_ff) + eps)
    inverse = (1.0 / (corrections + level)).astype(jnp.bfloat16)
    inverse = for_each(inverse, ("dp_0", "dp_1"))
    inverse = for_each(inverse, "dp_2").swapaxes(0, 1).reshape(width_d, width_ff)
    root = math.sqrt(width_d * width_ff)
    slot_scores = scored(grad, hid, inverse, all_grad, all_hid) / root
    returned = traded(slot_scores.reshape(experts, capacity, -1), "expert")
    queries = all_grad.shape[0]
    scores = jnp.take(returned.reshape(-1, queries), slots, axis=0).reshape(tok_rows, top, queries)
    return (scores, corrections[None])


def solution(mesh):
    torus = Mesh(
        mesh.devices.reshape(mesh.shape["expert"], 4, 2, 2), ("expert", "dp_0", "dp_1", "dp_2")
    )
    placed = (
        P(EXPERT_DP, None, None),
        P(EXPERT_DP, None),
        P(EXPERT_DP, None),
        P(EXPERT_DP, None),
        P("expert", None, None),
        P("expert", None, None),
        P("expert", DP, None),
        P("expert", DP, None),
        P("expert", DP),
        P("expert"),
    )
    return jax.shard_map(
        body,
        mesh=torus,
        in_specs=placed,
        out_specs=(P(EXPERT_DP, None, None), P("expert", DP, None)),
        check_vma=False,
    )
```

time: 291 us -> 202 us (0.69)
  blocking collectives: 86.3 us -> 6.26 us
  matrix products: 97.3 us -> 18.3 us
  waiting for transfers between devices: 35.2 us -> 81.5 us
  Pallas kernels: 0 us -> 25.9 us
  other arithmetic: 22.5 us -> 11.7 us
  starting transfers between devices: 23.3 us -> 30.3 us
    dot_general x20 -> x5, matrix products: 92.7 us -> 13.7 us  [the longest x1 6.88 us: body(): jnp.dot(held[:, width_ff:], rotate_gradient, preferred_element_type=jnp.f...]
    all_to_all x3 -> x1, blocking collectives: 59.3 us -> 6.26 us  [traded(): return lax.all_to_all(blocks, axis, split_axis=0, concat_axis=0, tiled=True)]
    all_to_all x5 -> x6, waiting for transfers between devices: 35.2 us -> 81.5 us  [traded(): return lax.all_to_all(blocks, axis, split_axis=0, concat_axis=0, tiled=True)]
    all_gather x1 -> x0, blocking collectives: 27 us -> none  [in_one_piece(): out = lax.all_gather(both, axis, axis=dim, tiled=True)]
    pallas_call x0 -> x1, Pallas kernels: none -> 25.9 us  [scored(): pl.pallas_call(functools.partial(score_kernel, group), grid=(queries // g...]
    all_to_all x5 -> x6, starting transfers between devices: 23.3 us -> 30.3 us  [traded(): return lax.all_to_all(blocks, axis, split_axis=0, concat_axis=0, tiled=True)]
    scatter x1 -> x0, other arithmetic: 4.55 us -> none  [body(): send_grad = jnp.zeros((experts * capacity, width_d), jnp.bfloat16).at[slo...]
  transfers between devices with their start and end apart: 5 -> 6, of which waited for: 4 -> 6; matrix products, arithmetic and copies ran while one was open for 7% -> 7% of each run, Pallas kernels for 0% -> 0%
where the time goes in v1:
time: 202 us; the launch traced here: 201 us
  waiting for transfers between devices  81.5 us (40%)
  starting transfers between devices  30.3 us (15%)
  Pallas kernels  25.9 us (13%)
  local copies, waits for them, and re-layouts  24.2 us (12%)
  matrix products  18.3 us (9%)
  other arithmetic  11.7 us (6%)
  blocking collectives  6.26 us (3%)
  between operations  2.84 us (1%)
    all_to_all x6, waiting for transfers between devices, traded(): return lax.all_to_all(blocks, axis, split_axis=0, concat_axis=0, tiled=True)  81.5 us
    all_to_all x6, starting transfers between devices, traded(): return lax.all_to_all(blocks, axis, split_axis=0, concat_axis=0, tiled=True)  30.3 us
    pallas_call x1, Pallas kernels, scored(): pl.pallas_call(functools.partial(score_kernel, group), grid=(queries // g...  25.9 us
    dot_general x1, matrix products, body(): jnp.dot(held[:, width_ff:], rotate_gradient, preferred_element_type=jnp.f...  6.88 us
    all_to_all x1, blocking collectives, traded(): return lax.all_to_all(blocks, axis, split_axis=0, concat_axis=0, tiled=True)  6.26 us
    mul x3, local copies, waits for them, and re-layouts, body(): route_weight[:, :, None] * token_grad[:, None, :].astype(jnp.float32)  4.72 us
    dot_general x1, matrix products, body(): jnp.dot(query_g, rotate_gradient, preferred_element_type=jnp.float32)  4.61 us
  transfers between devices with their start and end apart: 6, of which 6 were waited for; matrix products, arithmetic and copies ran while one was open for 7% of the time, Pallas kernels for 0%

profile of v1, /device:TPU:0, one launch (start us, length us, event | category | flops | bytes accessed | tf_op | source)
XLA Modules:
  0.0 201.1 jit_solution(14990934218129169887)
XLA Ops:
  0.6 0.0 copy-start
  0.6 0.9 copy.39
  1.5 0.1 reshape.153
  1.7 0.1 eq.39
  1.8 0.6 reduce-window.6
  2.4 0.2 slice_reduce_fusion.1
  2.7 0.1 fusion.21
  2.8 0.8 copy.42
  3.6 0.1 mul.76
  3.7 1.9 reshape.155
  5.6 2.1 %mul.78 = f32[128,2,2048]{2,1,0:T(2,128)S(1)} broadcast(bf16[128,2048]{1,0:T(8,128)(2,1)} %param.11), dimensions={0,2} | broadcast | bytes 2621440 | tf_op jit(solution)/shard_map/mul | solution.py:90
  7.7 2.5 %mul.79 = f32[256,2048]{1,0:T(8,128)} reshape(f32[128,2,2048]{2,1,0:T(2,128)S(1)} %mul.78) | data formatting | bytes 4194304 | tf_op jit(solution)/shard_map/mul | solution.py:90
  10.2 0.0 copy-start.3
  10.2 1.8 multiply_convert_fusion.1
  12.0 0.0 copy-done.3
  12.0 2.1 %convolution_convert_fusion = bf16[384,2816]{1,0:T(8,128)(2,1)} fusion(bf16[256,2048]{1,0:T(8,128)(2,1)S(1)} %multiply_convert_fusion.1, bf16[256,768]{1,0:T(8,128)(2,1)S(1)} %copy-done.3, s32[256]{0:T(256)S(1)} %multiply_add_fusion), kind=kOutput, calls=%fused_computation.5 | convolution fusion | flops 557711360 | bytes 3605504 | tf_op jit(solution)/shard_map/dot_general | solution.py:99
  14.1 7.9 %all-to-all-start = ((bf16[8,48,2816]{2,1,0:T(8,128)(2,1)}), bf16[8,48,2816]{2,1,0:T(8,128)(2,1)S(1)}, u32[]{:S(2)}, u32[]{:S(2)}) async-start(bf16[8,48,2816]{2,1,0:T(8,128)(2,1)} %bitcast.2), calls=%async_computation | async-start | bytes 4325376 | tf_op jit(solution)/shard_map/all_to_all | solution.py:65
  22.7 0.0 copy-done
  22.7 1.0 fusion.11
  23.7 4.6 %fusion = f32[1,2048]{1,0:T(1,128)S(1)} fusion(bf16[1,2048,2048]{2,1,0:T(8,128)(2,1)} %param.14, pred[]{:T(512)} %bitcast.10, bf16[1,8,2048]{2,1,0:T(8,128)(2,1)} %param.17, s32[]{:T(128)} %bitcast.11), kind=kOutput, calls=%fused_computation.1 | convolution fusion | flops 8390656 | bytes 8406016 | tf_op jit(solution)/shard_map/dot_general | solution.py:106
  28.3 25.9 %all-to-all-done = bf16[8,48,2816]{2,1,0:T(8,128)(2,1)S(1)} async-done(((bf16[8,48,2816]{2,1,0:T(8,128)(2,1)}), bf16[8,48,2816]{2,1,0:T(8,128)(2,1)S(1)}, u32[]{:S(2)}, u32[]{:S(2)}) %all-to-all-start) | async-done | bytes 2162720 | tf_op jit(solution)/shard_map/all_to_all | solution.py:65
  54.2 0.0 copy-start.1
  54.2 1.3 copy-done.1
  55.5 1.9 convert_reduce_fusion.2
  57.5 0.0 copy-done.2
  57.5 6.9 %convert_reduce_fusion = (f32[384]{0:T(512)S(1)}, bf16[384,2048]{1,0:T(8,128)(2,1)S(1)}) fusion(bf16[1,2048,2048]{2,1,0:T(8,128)(2,1)} %param.14, bf16[384,2816]{1,0:T(8,128)(2,1)S(1)} %bitcast.62), kind=kOutput, calls=%fused_computation.8 | convolution fusion | flops 3225943552 | bytes 11535872 | tf_op jit(solution)/shard_map/dot_general | solution.py:111
  64.3 1.9 convolution_convert_fusion.1
  66.2 2.0 copy.50
  68.2 5.2 %all-to-all-start.1 = ((bf16[2,8,128,768]{3,2,1,0:T(8,128)(2,1)}), bf16[2,8,128,768]{3,2,1,0:T(8,128)(2,1)}, u32[]{:S(2)}, u32[]{:S(2)}) async-start(bf16[2,8,128,768]{3,2,1,0:T(8,128)(2,1)} %bitcast.56), calls=%async_computation.1 | async-start | bytes 6291456 | tf_op jit(solution)/shard_map/all_to_all | solution.py:65
  73.4 0.6 multiply_reduce_fusion
  74.0 0.6 broadcast_in_dim.56
  74.7 2.4 %all-to-all-done.1 = bf16[2,8,128,768]{3,2,1,0:T(8,128)(2,1)} async-done(((bf16[2,8,128,768]{3,2,1,0:T(8,128)(2,1)}), bf16[2,8,128,768]{3,2,1,0:T(8,128)(2,1)}, u32[]{:S(2)}, u32[]{:S(2)}) %all-to-all-start.1) | async-done | bytes 3145760 | tf_op jit(solution)/shard_map/all_to_all | solution.py:65
  77.1 0.8 broadcast_in_dim.57
  77.9 4.9 %all-to-all-start.3 = ((f32[16,1,2944]{2,1,0:T(1,128)}), f32[16,1,2944]{2,1,0:T(1,128)S(1)}, u32[]{:S(2)}, u32[]{:S(2)}) async-start(f32[16,1,2944]{2,1,0:T(1,128)} %broadcast_in_dim.57), calls=%async_computation.3 | async-start | bytes 376832 | tf_op jit(solution)/shard_map/all_to_all | solution.py:65
  82.8 4.0 %reduce_sum.72 = bf16[8,128,768]{2,1,0:T(8,128)(2,1)} reduce(bf16[2,8,128,768]{3,2,1,0:T(8,128)(2,1)} %all-to-all-done.1, bf16[]{:T(256)} %constant.58.clone.1), dimensions={0}, to_apply=%region_3.4 | reduce | flops 786432 | bytes 4718594 | tf_op jit(solution)/shard_map/reduce_sum | solution.py:126
  86.8 3.0 %all-to-all-done.3 = f32[16,1,2944]{2,1,0:T(1,128)S(1)} async-done(((f32[16,1,2944]{2,1,0:T(1,128)}), f32[16,1,2944]{2,1,0:T(1,128)S(1)}, u32[]{:S(2)}, u32[]{:S(2)}) %all-to-all-start.3) | async-done | bytes 188448 | tf_op jit(solution)/shard_map/all_to_all | solution.py:65
  89.7 4.3 %all-to-all-start.2 = ((bf16[8,128,768]{2,1,0:T(8,128)(2,1)}), bf16[8,128,768]{2,1,0:T(8,128)(2,1)}, u32[]{:S(2)}, u32[]{:S(2)}) async-start(bf16[8,128,768]{2,1,0:T(8,128)(2,1)} %reduce_sum.72), calls=%async_computation.2 | async-start | bytes 3145728 | tf_op jit(solution)/shard_map/all_to_all | solution.py:65
  94.7 0.7 slice_reduce_fusion
  96.0 22.6 %all-to-all-done.2 = bf16[8,128,768]{2,1,0:T(8,128)(2,1)} async-done(((bf16[8,128,768]{2,1,0:T(8,128)(2,1)}), bf16[8,128,768]{2,1,0:T(8,128)(2,1)}, u32[]{:S(2)}, u32[]{:S(2)}) %all-to-all-start.2) | async-done | bytes 1572896 | tf_op jit(solution)/shard_map/all_to_all | solution.py:65
  118.7 1.7 convert_reduce_fusion.1
  120.3 0.8 multiply_bitcast_fusion
  121.1 1.3 broadcast_in_dim.58
  122.4 4.5 %all-to-all-start.4 = ((bf16[8,128,768]{2,1,0:T(8,128)(2,1)}), bf16[8,128,768]{2,1,0:T(8,128)(2,1)}, u32[]{:S(2)}, u32[]{:S(2)}) async-start(bf16[8,128,768]{2,1,0:T(8,128)(2,1)} %broadcast_in_dim.58), calls=%async_computation.4 | async-start | bytes 3145728 | tf_op jit(solution)/shard_map/all_to_all | solution.py:65
  126.9 0.8 reduce_sum.71
  127.6 0.0 copy-done.4
  127.6 0.7 copy.47
  128.4 1.0 mul.85
  129.3 0.9 copy.41
  130.3 19.8 %all-to-all-done.4 = bf16[8,128,768]{2,1,0:T(8,128)(2,1)} async-done(((bf16[8,128,768]{2,1,0:T(8,128)(2,1)}), bf16[8,128,768]{2,1,0:T(8,128)(2,1)}, u32[]{:S(2)}, u32[]{:S(2)}) %all-to-all-start.4) | async-done | bytes 1572896 | tf_op jit(solution)/shard_map/all_to_all | solution.py:65
  150.2 1.7 broadcast_in_dim.59
  151.9 6.3 %all_to_all.35 = bf16[2,8,128,768]{3,2,1,0:T(8,128)(2,1)S(1)} all-to-all(bf16[2,8,128,768]{3,2,1,0:T(8,128)(2,1)S(1)} %broadcast_in_dim.59), channel_id=1, replica_groups=mesh['expert'=8,'dp_0'=4,'dp_1'=2,'dp_2'=2] {'dp_2'}, dimensions={0} | all-to-all | bytes 6291456 | tf_op jit(solution)/shard_map/all_to_all | solution.py:65
  158.2 2.0 copy.44
  160.1 25.9 %shard_map.113 = f32[384,128]{1,0:T(8,128)S(1)} custom-call(bf16[384,2048]{1,0:T(8,128)(2,1)S(1)} %get-tuple-element.27.g_ref, bf16[384,768]{1,0:T(8,128)(2,1)S(1)} %get-tuple-element.29.h_ref, bf16[2048,768]{1,0:T(8,128)(2,1)} %bitcast.58, f32[16,1,2048]{2,1,0:T(1,128)S(1)} %slice.58.qg_ref, f32[16,1,768]{2,1,0:T(1,128)S(1)} %slice.59.qh_ref), custom_call_target="tpu_custom_call" | custom-call | tf_op jit(solution)/shard_map/pallas_call | solution.py:44
  186.1 0.1 copy.45
  186.2 0.7 reshape.238
  186.9 3.6 %all-to-all-start.6 = ((f32[8,1,768]{2,1,0:T(1,128)}), f32[8,1,768]{2,1,0:T(1,128)S(1)}, u32[]{:S(2)}, u32[]{:S(2)}) async-start(f32[8,1,768]{2,1,0:T(1,128)} %reshape.238), calls=%async_computation.6 | async-start | bytes 49152 | tf_op jit(solution)/shard_map/all_to_all | solution.py:65
  190.6 7.7 %all-to-all-done.6 = f32[8,1,768]{2,1,0:T(1,128)S(1)} async-done(((f32[8,1,768]{2,1,0:T(1,128)}), f32[8,1,768]{2,1,0:T(1,128)S(1)}, u32[]{:S(2)}, u32[]{:S(2)}) %all-to-all-start.6) | async-done | bytes 24608 | tf_op jit(solution)/shard_map/all_to_all | solution.py:65
  198.3 0.5 broadcast.202
  198.8 0.7 reduce.6
  199.5 0.1 reshape.239
  199.6 0.1 copy.46
  199.7 0.7 gather_fusion
  200.4 0.1 copy.48
  200.5 0.6 broadcast_select_fusion.1
  (16 shorter events, 0.2 us)
Async XLA Ops:
  0.6 22.0 %copy-start = (bf16[1,768,768]{2,1,0:T(8,128)(2,1)S(1)}, bf16[1,768,768]{2,1,0:T(8,128)(2,1)}, u32[]{:S(2)}) copy-start(bf16[1,768,768]{2,1,0:T(8,128)(2,1)} %param.15) | copy-start | bytes 3538948
  10.2 1.8 copy-start.3
  14.1 40.1 %all-to-all-start = ((bf16[8,48,2816]{2,1,0:T(8,128)(2,1)}), bf16[8,48,2816]{2,1,0:T(8,128)(2,1)S(1)}, u32[]{:S(2)}, u32[]{:S(2)}) async-start(bf16[8,48,2816]{2,1,0:T(8,128)(2,1)} %bitcast.2), calls=%async_computation | async-start | bytes 4325376 | tf_op jit(solution)/shard_map/all_to_all | solution.py:65
  54.2 1.4 copy-start.1
  55.5 1.9 copy-start.2
  68.2 8.9 %all-to-all-start.1 = ((bf16[2,8,128,768]{3,2,1,0:T(8,128)(2,1)}), bf16[2,8,128,768]{3,2,1,0:T(8,128)(2,1)}, u32[]{:S(2)}, u32[]{:S(2)}) async-start(bf16[2,8,128,768]{3,2,1,0:T(8,128)(2,1)} %bitcast.56), calls=%async_computation.1 | async-start | bytes 6291456 | tf_op jit(solution)/shard_map/all_to_all | solution.py:65
  77.9 11.8 %all-to-all-start.3 = ((f32[16,1,2944]{2,1,0:T(1,128)}), f32[16,1,2944]{2,1,0:T(1,128)S(1)}, u32[]{:S(2)}, u32[]{:S(2)}) async-start(f32[16,1,2944]{2,1,0:T(1,128)} %broadcast_in_dim.57), calls=%async_computation.3 | async-start | bytes 376832 | tf_op jit(solution)/shard_map/all_to_all | solution.py:65
  89.7 28.9 %all-to-all-start.2 = ((bf16[8,128,768]{2,1,0:T(8,128)(2,1)}), bf16[8,128,768]{2,1,0:T(8,128)(2,1)}, u32[]{:S(2)}, u32[]{:S(2)}) async-start(bf16[8,128,768]{2,1,0:T(8,128)(2,1)} %reduce_sum.72), calls=%async_computation.2 | async-start | bytes 3145728 | tf_op jit(solution)/shard_map/all_to_all | solution.py:65
  121.1 6.5 %copy-start.4 = (s32[128,2]{0,1:T(2,128)S(1)}, s32[128,2]{0,1:T(2,128)}, u32[]{:S(2)}) copy-start(s32[128,2]{0,1:T(2,128)} %param.12) | copy-start | bytes 3076
  122.4 27.8 %all-to-all-start.4 = ((bf16[8,128,768]{2,1,0:T(8,128)(2,1)}), bf16[8,128,768]{2,1,0:T(8,128)(2,1)}, u32[]{:S(2)}, u32[]{:S(2)}) async-start(bf16[8,128,768]{2,1,0:T(8,128)(2,1)} %broadcast_in_dim.58), calls=%async_computation.4 | async-start | bytes 3145728 | tf_op jit(solution)/shard_map/all_to_all | solution.py:65
  186.9 11.3 %all-to-all-start.6 = ((f32[8,1,768]{2,1,0:T(1,128)}), f32[8,1,768]{2,1,0:T(1,128)S(1)}, u32[]{:S(2)}, u32[]{:S(2)}) async-start(f32[8,1,768]{2,1,0:T(1,128)} %reshape.238), calls=%async_computation.6 | async-start | bytes 49152 | tf_op jit(solution)/shard_map/all_to_all | solution.py:65

commit v2 on v1

v2 whole, which is shorter than its diff:
```python
import functools
import math

import jax
import jax.numpy as jnp
from jax import lax
from jax.experimental import pallas as pl
from jax.experimental.pallas import tpu as pltpu
from jax.sharding import Mesh
from jax.sharding import PartitionSpec as P

DP = ("dp_0", "dp_1", "dp_2")
EXPERT_DP = ("expert", "dp_0", "dp_1", "dp_2")

eps = 1e-06


MESH = pl.DeviceIdType.MESH
CHUNK = 128


def back_kernel(
    scale,
    root,
    g_ref,
    h_ref,
    small_ref,
    slots_ref,
    damp_ref,
    out_ref,
    corr_ref,
    gsq,
    hsq,
    small,
    part,
    nearby,
    summed,
    far,
    inv,
    acc,
    ret_out,
    ret_in,
    small_s,
    small_r,
    core_s,
    core_r,
    rs_s,
    rs_r,
    ag_s,
    ag_r,
    cg_s,
    cg_r,
    ret_s,
    ret_r,
):
    e = lax.axis_index("expert")
    x = lax.axis_index("dp_0")
    z = lax.axis_index("dp_1")
    k = lax.axis_index("dp_2")
    xz = x * 2 + z
    chips = part.shape[2]
    experts = ret_out.shape[0]
    capacity = ret_out.shape[1]
    rows, width_d = g_ref.shape
    width_ff = h_ref.shape[1]
    chunks = width_ff // CHUNK
    bf16, f32 = jnp.bfloat16, jnp.float32

    def dp_id(index):
        return {"dp_0": index // 4, "dp_1": lax.rem(index // 2, 2), "dp_2": lax.rem(index, 2)}

    def chip_id(index):
        return {"dp_0": index // 2, "dp_1": lax.rem(index, 2)}

    me = xz * 2 + k
    barrier = pltpu.get_barrier_semaphore()

    def greet_dp(d, _):
        pl.semaphore_signal(
            barrier, 1, device_id=dp_id(lax.rem(me + d, 2 * chips)), device_id_type=MESH
        )
        return 0

    def greet_expert(d, _):
        pl.semaphore_signal(
            barrier, 1, device_id={"expert": lax.rem(e + d, experts)}, device_id_type=MESH
        )
        return 0

    lax.fori_loop(1, 2 * chips, greet_dp, 0)
    lax.fori_loop(1, experts, greet_expert, 0)

    gsq[...] = jnp.square(g_ref[...].astype(f32)).astype(bf16)
    hsq[...] = jnp.square(h_ref[...].astype(f32)).astype(bf16)
    acc[...] = jnp.zeros_like(acc)
    pl.semaphore_wait(barrier, 2 * chips - 1 + experts - 1)

    def core_copy(c):
        return pltpu.make_async_remote_copy(
            part.at[c, 1 - k],
            nearby.at[c],
            core_s.at[c],
            core_r.at[c],
            device_id={"dp_2": 1 - k},
            device_id_type=MESH,
        )

    def rs_copy(c, d):
        to = lax.rem(xz + d, chips)
        return pltpu.make_async_remote_copy(
            summed.at[c, to],
            far.at[c, d],
            rs_s.at[c, d],
            rs_r.at[c, d],
            device_id=chip_id(to),
            device_id_type=MESH,
        )

    def ag_copy(c, d):
        to = lax.rem(xz + d, chips)
        return pltpu.make_async_remote_copy(
            inv.at[c, k, xz],
            inv.at[c, k, xz],
            ag_s.at[c, d],
            ag_r.at[c, d],
            device_id=chip_id(to),
            device_id_type=MESH,
        )

    def ag_arrival(c, d):
        origin = lax.rem(xz + chips - d, chips)
        return pltpu.make_async_remote_copy(
            inv.at[c, k, origin],
            inv.at[c, k, origin],
            ag_s.at[c, d],
            ag_r.at[c, d],
            device_id=chip_id(origin),
            device_id_type=MESH,
        )

    def cg_copy(c, side):
        return pltpu.make_async_remote_copy(
            inv.at[c, side],
            inv.at[c, side],
            cg_s.at[c],
            cg_r.at[c],
            device_id={"dp_2": 1 - k},
            device_id_type=MESH,
        )

    def small_copy(d, slot):
        return pltpu.make_async_remote_copy(
            small.at[me],
            small.at[slot],
            small_s.at[d],
            small_r.at[d],
            device_id=dp_id(lax.rem(me + d, 2 * chips)),
            device_id_type=MESH,
        )

    def each(first, last, act):
        def once(d, _):
            act(d)
            return 0

        lax.fori_loop(first, last, once, 0)

    for pair in range(chunks // 2):
        both = lax.dot_general(
            hsq[:, pair * 2 * CHUNK : (pair + 1) * 2 * CHUNK],
            gsq[...],
            (((0,), (0,)), ((), ())),
            preferred_element_type=f32,
        ).astype(bf16)
        for half in range(2):
            for q in range(2 * chips):
                part[2 * pair + half, q % 2, q // 2] = both[
                    half * CHUNK : (half + 1) * CHUNK, q * CHUNK : (q + 1) * CHUNK
                ]
        for half in range(2):
            core_copy(2 * pair + half).start()

    row_g = jnp.sum(gsq[...].astype(f32), axis=1, keepdims=True)
    row_h = jnp.sum(hsq[...].astype(f32), axis=1, keepdims=True)
    own_sum = jnp.sum(row_g * row_h, axis=0, keepdims=True)
    place = lax.broadcasted_iota(jnp.int32, small_ref.shape, 0)
    small[me] = jnp.where(place == 22, jnp.broadcast_to(own_sum, small_ref.shape), small_ref[...])
    each(1, 2 * chips, lambda d: small_copy(d, me).start())

    def stage_one(c):
        core_copy(c).wait()
        summed[c] = (part[c, k].astype(f32) + nearby[c].astype(f32)).astype(bf16)
        each(1, chips, lambda d: rs_copy(c, d).start())

    def stage_two(c, level):
        each(1, chips, lambda d: rs_copy(c, d).wait_recv())
        total = summed[c, xz].astype(f32)
        for d in range(1, chips):
            total = total + far[c, d].astype(f32)
        block = total.T * scale
        corr_ref[:, c * CHUNK : (c + 1) * CHUNK] = block
        inv[c, k, xz] = (1.0 / (block + level)).astype(bf16)
        each(1, chips, lambda d: ag_copy(c, d).start())

    def stage_three(c):
        each(1, chips, lambda d: ag_arrival(c, d).wait_recv())
        cg_copy(c, k).start()

    def ready(c):
        cg_copy(c, 1 - k).wait_recv()

    lane = lax.broadcasted_iota(jnp.int32, acc.shape, 1)
    group = 4

    def score(pair, first, last):
        def step(t, _):
            parts = []
            for j in range(group):
                n = t * group + j
                pieces = []
                for q in range(2 * chips):
                    d = (q % chips) * 2 + q // chips
                    pieces.append(
                        g_ref[:, d * CHUNK : (d + 1) * CHUNK]
                        * small[n, d : d + 1, :].astype(bf16)
                    )
                parts.append(jnp.concatenate(pieces, axis=1))
            scaled = jnp.concatenate(parts, axis=0)
            weights = jnp.concatenate(
                [inv[2 * pair + half].reshape(width_d, CHUNK) for half in range(2)], axis=1
            )
            product = jnp.dot(scaled, weights, preferred_element_type=f32)
            total = acc[...]
            for j in range(group):
                n = t * group + j
                value = None
                for half in range(2):
                    c = 2 * pair + half
                    term = product[
                        j * rows : (j + 1) * rows, half * CHUNK : (half + 1) * CHUNK
                    ] * (
                        h_ref[:, c * CHUNK : (c + 1) * CHUNK].astype(f32)
                        * small[n, 16 + c : 17 + c, :]
                    )
                    value = term if value is None else value + term
                total = total + jnp.where(
                    lane == n, jnp.sum(value, axis=1, keepdims=True), 0.0
                )
            acc[...] = total
            return 0

        lax.fori_loop(first, last, step, 0)

    stage_one(0)
    stage_one(1)

    def small_arrival(d):
        small_copy(d, lax.rem(me + 2 * chips - d, 2 * chips)).wait_recv()

    each(1, 2 * chips, small_arrival)
    complete = small[0, 22:23, :]
    for n in range(1, 2 * chips):
        complete = complete + small[n, 22:23, :]
    level = damp_ref[...] * (complete * (scale / (width_d * width_ff)) + eps)

    stage_two(0, level)
    stage_one(2)
    stage_two(1, level)
    stage_one(3)
    stage_three(0)
    stage_two(2, level)
    stage_one(4)
    stage_three(1)
    stage_two(3, level)
    stage_one(5)
    ready(0)
    ready(1)
    score(0, 0, 2)
    stage_three(2)
    score(0, 2, 3)
    stage_two(4, level)
    score(0, 3, 4)
    stage_three(3)
    stage_two(5, level)
    ready(2)
    ready(3)
    score(1, 0, 2)
    stage_three(4)
    score(1, 2, 4)
    stage_three(5)
    ready(4)
    ready(5)
    score(2, 0, 4)

    ret_out[...] = (acc[...] / root).reshape(ret_out.shape)

    def ret_copy(d, slot):
        to = lax.rem(e + d, experts)
        return pltpu.make_async_remote_copy(
            ret_out.at[to],
            ret_in.at[slot],
            ret_s.at[d],
            ret_r.at[d],
            device_id={"expert": to},
            device_id_type=MESH,
        )

    each(1, experts, lambda d: ret_copy(d, e).start())
    ret_in[e] = ret_out[e]
    chosen = (
        slots_ref[...]
        == lax.broadcasted_iota(jnp.int32, (out_ref.shape[0], experts * capacity), 1)
    ).astype(f32)
    each(1, experts, lambda d: ret_copy(d, lax.rem(e + experts - d, experts)).wait_recv())
    out_ref[...] = jnp.dot(
        chosen,
        ret_in[...].reshape(experts * capacity, -1),
        preferred_element_type=f32,
        precision=lax.Precision.HIGHEST,
    )
    for c in range(chunks):
        each(1, chips, lambda d: rs_copy(c, d).wait_send())
        each(1, chips, lambda d: ag_copy(c, d).wait_send())
        cg_copy(c, k).wait_send()
    each(1, 2 * chips, lambda d: small_copy(d, me).wait_send())
    each(1, experts, lambda d: ret_copy(d, e).wait_send())


def back_half(grad, hid, small, slots, damp, experts, capacity, replicas):
    rows, width_d = grad.shape
    width_ff = hid.shape[1]
    chips = replicas // 2
    chunks = width_ff // CHUNK
    bf16, f32 = jnp.bfloat16, jnp.float32
    block = width_d // replicas
    dma = pltpu.SemaphoreType.DMA
    vmem = pl.BlockSpec(memory_space=pltpu.VMEM)
    return pl.pallas_call(
        functools.partial(
            back_kernel, 1.0 / (replicas * experts * capacity), math.sqrt(width_d * width_ff)
        ),
        out_shape=(
            jax.ShapeDtypeStruct((slots.shape[0], 128), f32),
            jax.ShapeDtypeStruct((block, width_ff), f32),
        ),
        in_specs=[vmem] * 5,
        out_specs=(vmem, vmem),
        scratch_shapes=[
            pltpu.VMEM((rows, width_d), bf16),
            pltpu.VMEM((rows, width_ff), bf16),
            pltpu.VMEM((replicas, *small.shape), f32),
            pltpu.VMEM((chunks, 2, chips, CHUNK, block), bf16),
            pltpu.VMEM((chunks, chips, CHUNK, block), bf16),
            pltpu.VMEM((chunks, chips, CHUNK, block), bf16),
            pltpu.VMEM((chunks, chips, CHUNK, block), bf16),
            pltpu.VMEM((chunks, 2, chips, block, CHUNK), bf16),
            pltpu.VMEM((rows, 128), f32),
            pltpu.VMEM((experts, capacity, 128), f32),
            pltpu.VMEM((experts, capacity, 128), f32),
            dma((replicas,)),
            dma((replicas,)),
            dma((chunks,)),
            dma((chunks,)),
            dma((chunks, chips)),
            dma((chunks, chips)),
            dma((chunks, chips)),
            dma((chunks, chips)),
            dma((chunks,)),
            dma((chunks,)),
            dma((experts,)),
            dma((experts,)),
        ],
        compiler_params=pltpu.CompilerParams(
            collective_id=0, has_side_effects=True, vmem_limit_bytes=60 * 1024 * 1024
        ),
    )(grad, hid, small, slots, damp)


def slot_index(routes_flat, experts, capacity):
    onehot = (routes_flat[:, None] == jnp.arange(experts, dtype=jnp.int32)[None, :]).astype(
        jnp.int32
    )
    before = jnp.cumsum(onehot, axis=0) - onehot
    return routes_flat * capacity + jnp.sum(before * onehot, axis=1)


def traded(blocks, axis):
    return lax.all_to_all(blocks, axis, split_axis=0, concat_axis=0, tiled=True)


def body(
    token_hidden,
    token_grad,
    routes,
    route_weight,
    gradient_eigenbasis,
    basis_hidden,
    query_hidden,
    query_grad,
    query_ids,
    damping,
):
    experts = lax.axis_size("expert")
    replicas = lax.axis_size(DP)
    tok_rows, top, width_ff = token_hidden.shape
    width_d = token_grad.shape[1]
    capacity = tok_rows * top * 3 // (2 * experts)
    slots = slot_index(routes.reshape(-1), experts, capacity)
    weighted = (route_weight[:, :, None] * token_grad[:, None, :].astype(jnp.float32)).astype(
        jnp.bfloat16
    )
    rows = jnp.concatenate(
        (token_hidden.reshape(-1, width_ff), weighted.reshape(-1, width_d)), axis=1
    )
    chosen = (slots[None, :] == jnp.arange(experts * capacity, dtype=jnp.int32)[:, None]).astype(
        jnp.bfloat16
    )
    sent = jnp.dot(chosen, rows, preferred_element_type=jnp.float32).astype(jnp.bfloat16)
    held = traded(sent.reshape(experts, capacity, -1), "expert").reshape(experts * capacity, -1)
    rotate_h = basis_hidden[0]
    rotate_gradient = gradient_eigenbasis[0]
    picks = query_ids[0]
    query_g = jnp.take(query_grad[0], picks, axis=0)
    query_h = jnp.take(query_hidden[0], picks, axis=0)
    query_g_rot = jnp.dot(query_g, rotate_gradient, preferred_element_type=jnp.float32)
    query_h_rot = jnp.dot(query_h, rotate_h, preferred_element_type=jnp.float32)
    hid = jnp.dot(held[:, :width_ff], rotate_h, preferred_element_type=jnp.float32).astype(
        jnp.bfloat16
    )
    grad = jnp.dot(held[:, width_ff:], rotate_gradient, preferred_element_type=jnp.float32).astype(
        jnp.bfloat16
    )
    small = jnp.concatenate(
        (
            query_g_rot.astype(jnp.bfloat16).astype(jnp.float32).reshape(-1, 128),
            query_h_rot.astype(jnp.bfloat16).astype(jnp.float32).reshape(-1, 128),
            jnp.zeros((2, 128), jnp.float32),
        ),
        axis=0,
    )
    damp = jnp.broadcast_to(damping[:, None], (1, 128))
    picked, corrections = back_half(
        grad, hid, small, slots[:, None], damp, experts, capacity, replicas
    )
    scores = picked[:, :replicas].reshape(tok_rows, top, replicas)
    return (scores, corrections[None])


def solution(mesh):
    torus = Mesh(
        mesh.devices.reshape(mesh.shape["expert"], 4, 2, 2), ("expert", "dp_0", "dp_1", "dp_2")
    )
    placed = (
        P(EXPERT_DP, None, None),
        P(EXPERT_DP, None),
        P(EXPERT_DP, None),
        P(EXPERT_DP, None),
        P("expert", None, None),
        P("expert", None, None),
        P("expert", DP, None),
        P("expert", DP, None),
        P("expert", DP),
        P("expert"),
    )
    return jax.shard_map(
        body,
        mesh=torus,
        in_specs=placed,
        out_specs=(P(EXPERT_DP, None, None), P("expert", DP, None)),
        check_vma=False,
    )
```

time: 202 us -> 138 us (0.68)
  waiting for transfers between devices: 81.5 us -> 23.4 us
  Pallas kernels: 25.9 us -> 70.8 us
  starting transfers between devices: 30.3 us -> 8.03 us
  local copies, waits for them, and re-layouts: 24.2 us -> 12.5 us
  other arithmetic: 11.7 us -> 3.19 us
  blocking collectives: 6.26 us -> 0 us
    all_to_all x6 -> x1, waiting for transfers between devices: 81.5 us -> 23.4 us  [traded(): return lax.all_to_all(blocks, axis, split_axis=0, concat_axis=0, tiled=True)]
    pallas_call x1, Pallas kernels: 25.9 us -> 70.8 us  [back_half(): pl.pallas_call(functools.partial(back_kernel, 1.0 / (replicas * experts *...]
    all_to_all x6 -> x1, starting transfers between devices: 30.3 us -> 8.03 us  [traded(): return lax.all_to_all(blocks, axis, split_axis=0, concat_axis=0, tiled=True)]
    reduce_sum x4 -> x0, other arithmetic: 6.97 us -> none  [the longest x1 4.02 us: body(): traded(blocks, 'dp_2').astype(jnp.float32).sum(axis=0).astype(jnp.bfloat16)]
    all_to_all x1 -> x0, blocking collectives: 6.26 us -> none  [traded(): return lax.all_to_all(blocks, axis, split_axis=0, concat_axis=0, tiled=True)]
    broadcast_in_dim x4 -> x2, local copies, waits for them, and re-layouts: 4.41 us -> 0.59 us  [the longest x1 0.59 us: body(): damp = jnp.broadcast_to(damping[:, None], (1, 128))]
    reshape x2 -> x0, local copies, waits for them, and re-layouts: 2.07 us -> none  [the longest x1 1.99 us: body(): blocks = partial.reshape(chips, 2, part, width_ff).swapaxes(0, 1)]
    unnamed x14 -> x10, local copies, waits for them, and re-layouts: 3.86 us -> 4.36 us
  transfers between devices with their start and end apart: 6 -> 1, of which waited for: 6 -> 1; matrix products, arithmetic and copies ran while one was open for 7% -> 5% of each run, Pallas kernels for 0% -> 0%
where the time goes in v2:
time: 138 us; the launch traced here: 137 us
  Pallas kernels  70.8 us (51%)
  waiting for transfers between devices  23.4 us (17%)
  matrix products  17.2 us (12%)
  local copies, waits for them, and re-layouts  12.5 us (9%)
  starting transfers between devices  8.03 us (6%)
  other arithmetic  3.19 us (2%)
  between operations  2.07 us (1%)
    pallas_call x1, Pallas kernels, back_half(): pl.pallas_call(functools.partial(back_kernel, 1.0 / (replicas * experts *...  70.8 us
    all_to_all x1, waiting for transfers between devices, traded(): return lax.all_to_all(blocks, axis, split_axis=0, concat_axis=0, tiled=True)  23.4 us
    dot_general x1, matrix products, body(): jnp.dot(held[:, width_ff:], rotate_gradient, preferred_element_type=jnp.f...  8.03 us
    all_to_all x1, starting transfers between devices, traded(): return lax.all_to_all(blocks, axis, split_axis=0, concat_axis=0, tiled=True)  8.03 us
    mul x3, local copies, waits for them, and re-layouts, body(): route_weight[:, :, None] * token_grad[:, None, :].astype(jnp.float32)  4.73 us
    dot_general x1, matrix products, body(): jnp.dot(query_g, rotate_gradient, preferred_element_type=jnp.float32)  4.6 us
    unnamed x10, local copies, waits for them, and re-layouts  4.36 us
  transfers between devices with their start and end apart: 1, of which 1 were waited for; matrix products, arithmetic and copies ran while one was open for 5% of the time, Pallas kernels for 0%

profile of v2, /device:TPU:0, one launch (start us, length us, event | category | flops | bytes accessed | tf_op | source)
XLA Modules:
  0.0 137.1 jit_solution(15111488709330698381)
XLA Ops:
  0.6 0.0 copy-start
  0.6 0.9 copy.21
  1.5 0.1 eq.39
  1.7 0.1 reshape.132
  1.8 2.1 %mul.50 = f32[128,2,2048]{2,1,0:T(2,128)S(1)} broadcast(bf16[128,2048]{1,0:T(8,128)(2,1)} %param.11), dimensions={0,2} | broadcast | bytes 2621440 | tf_op jit(solution)/shard_map/mul | solution.py:409
  3.9 0.0 copy-start.2
  3.9 2.5 %mul.51 = f32[256,2048]{1,0:T(8,128)} reshape(f32[128,2,2048]{2,1,0:T(2,128)S(1)} %mul.50) | data formatting | bytes 4194304 | tf_op jit(solution)/shard_map/mul | solution.py:409
  6.4 0.0 copy-done.2
  6.4 0.1 copy.23
  6.5 0.1 mul.48
  6.7 1.1 reshape.134
  7.8 0.6 reduce-window.6
  8.4 0.2 slice_reduce_fusion
  8.7 0.1 fusion.22
  8.8 1.8 %multiply_convert_fusion = bf16[256,2048]{1,0:T(8,128)(2,1)S(1)} fusion(f32[256,2048]{1,0:T(8,128)} %mul.51, f32[256]{0:T(256)S(1)} %mul.48), kind=kLoop, calls=%fused_computation.6 | loop fusion | flops 1048576 | bytes 3146752 | tf_op jit(solution)/shard_map/convert_element_type | solution.py:409
  10.6 2.1 %convolution_convert_fusion = bf16[384,2816]{1,0:T(8,128)(2,1)} fusion(bf16[256,2048]{1,0:T(8,128)(2,1)S(1)} %multiply_convert_fusion, bf16[256,768]{1,0:T(8,128)(2,1)S(1)} %reshape.134, s32[256]{0:T(256)S(1)} %multiply_add_fusion), kind=kOutput, calls=%fused_computation.4 | convolution fusion | flops 557711360 | bytes 3605504 | tf_op jit(solution)/shard_map/dot_general | solution.py:418
  12.7 0.0 copy-start.1
  12.7 8.0 %all-to-all-start = ((bf16[8,48,2816]{2,1,0:T(8,128)(2,1)}), bf16[8,48,2816]{2,1,0:T(8,128)(2,1)S(1)}, u32[]{:S(2)}, u32[]{:S(2)}) async-start(bf16[8,48,2816]{2,1,0:T(8,128)(2,1)} %bitcast.2), calls=%async_computation | async-start | bytes 4325376 | tf_op jit(solution)/shard_map/all_to_all | solution.py:388
  21.3 0.0 copy-done.1
  21.4 0.1 copy.24
  21.5 0.1 mul.55
  21.6 0.8 copy.25.slots_ref
  23.1 0.1 pad.6.clone
  23.2 0.0 copy-done
  23.2 1.0 fusion.14
  24.2 4.6 %fusion = f32[1,2048]{1,0:T(1,128)S(1)} fusion(bf16[1,2048,2048]{2,1,0:T(8,128)(2,1)} %param.14, pred[]{:T(512)} %bitcast.7, bf16[1,8,2048]{2,1,0:T(8,128)(2,1)} %param.17, s32[]{:T(128)} %bitcast.8), kind=kOutput, calls=%fused_computation | convolution fusion | flops 8390656 | bytes 8406016 | tf_op jit(solution)/shard_map/dot_general | solution.py:425
  28.8 0.7 maximum_maximum_fusion.small_ref
  29.5 23.4 %all-to-all-done = bf16[8,48,2816]{2,1,0:T(8,128)(2,1)S(1)} async-done(((bf16[8,48,2816]{2,1,0:T(8,128)(2,1)}), bf16[8,48,2816]{2,1,0:T(8,128)(2,1)S(1)}, u32[]{:S(2)}, u32[]{:S(2)}) %all-to-all-start) | async-done | bytes 2162720 | tf_op jit(solution)/shard_map/all_to_all | solution.py:388
  52.9 8.0 %fusion.4.g_ref = bf16[384,2048]{1,0:T(8,128)(2,1)} fusion(bf16[1,2048,2048]{2,1,0:T(8,128)(2,1)} %param.14, bf16[384,2816]{1,0:T(8,128)(2,1)S(1)} %bitcast.49), kind=kOutput, calls=%fused_computation.5 | convolution fusion | flops 3222011904 | bytes 11534336 | tf_op jit(solution)/shard_map/dot_general | solution.py:430
  60.9 1.4 %convolution_convert_fusion.1.h_ref = bf16[384,768]{1,0:T(8,128)(2,1)} fusion(bf16[1,768,768]{2,1,0:T(8,128)(2,1)S(1)} %copy-done, bf16[384,2816]{1,0:T(8,128)(2,1)S(1)} %bitcast.50), kind=kOutput, calls=%fused_computation.11 | convolution fusion | flops 453279744 | bytes 2359296 | tf_op jit(solution)/shard_map/dot_general | solution.py:427
  62.3 0.6 broadcast_in_dim.49.damp_ref
  62.9 70.8 %shard_map.113 = (f32[256,128]{1,0:T(8,128)}, f32[128,768]{1,0:T(8,128)}) custom-call(bf16[384,2048]{1,0:T(8,128)(2,1)} %fusion.4.g_ref, bf16[384,768]{1,0:T(8,128)(2,1)} %convolution_convert_fusion.1.h_ref, f32[24,128]{1,0:T(8,128)} %maximum_maximum_fusion.small_ref, s32[256,1]{1,0:T(8,128)} %copy.25.slots_ref, f32[1,128]{1,0:T(1,128)} %broadcast_in_dim.49.damp_ref), custom_call_target="tpu_custom_call" | custom-call | tf_op jit(solution)/shard_map/pallas_call | solution.py:338
  133.8 1.6 %copy.26 = f32[128,2,16]{0,2,1:T(8,128)} copy(f32[128,2,16]{2,1,0:T(2,128)} %bitcast.52) | data formatting | bytes 32768
  135.3 1.8 %copy.30 = f32[1,128,768]{2,1,0:T(8,128)} copy(f32[1,128,768]{2,1,0:T(8,128)} %bitcast.51) | data formatting | bytes 786432
  (9 shorter events, 0.1 us)
Async XLA Ops:
  0.6 22.6 %copy-start = (bf16[1,768,768]{2,1,0:T(8,128)(2,1)S(1)}, bf16[1,768,768]{2,1,0:T(8,128)(2,1)}, u32[]{:S(2)}) copy-start(bf16[1,768,768]{2,1,0:T(8,128)(2,1)} %param.15) | copy-start | bytes 3538948
  3.9 2.5 %copy-start.2 = (f32[128,2]{0,1:T(2,128)S(1)}, f32[128,2]{0,1:T(2,128)}, u32[]{:S(2)}) copy-start(f32[128,2]{0,1:T(2,128)} %param.13) | copy-start | bytes 3076
  12.7 8.7 %copy-start.1 = (s32[128,2]{0,1:T(2,128)S(1)}, s32[128,2]{0,1:T(2,128)}, u32[]{:S(2)}) copy-start(s32[128,2]{0,1:T(2,128)} %param.12) | copy-start | bytes 3076
  12.7 40.2 %all-to-all-start = ((bf16[8,48,2816]{2,1,0:T(8,128)(2,1)}), bf16[8,48,2816]{2,1,0:T(8,128)(2,1)S(1)}, u32[]{:S(2)}, u32[]{:S(2)}) async-start(bf16[8,48,2816]{2,1,0:T(8,128)(2,1)} %bitcast.2), calls=%async_computation | async-start | bytes 4325376 | tf_op jit(solution)/shard_map/all_to_all | solution.py:388

commit v3 on v2

--- a/solution.py
+++ b/solution.py
@@ -22,13 +22,26 @@
 def back_kernel(
     scale,
     root,
-    g_ref,
-    h_ref,
-    small_ref,
-    slots_ref,
+    routes_ref,
+    weight_ref,
+    hidden_ref,
+    grad_ref,
+    basis_g_ref,
+    basis_h_ref,
+    query_g_ref,
+    query_h_ref,
+    ids_ref,
     damp_ref,
     out_ref,
     corr_ref,
+    basis_g,
+    basis_h,
+    send_g,
+    send_h,
+    held_g,
+    held_h,
+    g_ref,
+    h_ref,
     gsq,
     hsq,
     small,
@@ -40,6 +53,11 @@
     acc,
     ret_out,
     ret_in,
+    basis_sem,
+    dg_s,
+    dg_r,
+    dh_s,
+    dh_r,
     small_s,
     small_r,
     core_s,
@@ -89,11 +107,106 @@
 
     lax.fori_loop(1, 2 * chips, greet_dp, 0)
     lax.fori_loop(1, experts, greet_expert, 0)
-
-    gsq[...] = jnp.square(g_ref[...].astype(f32)).astype(bf16)
-    hsq[...] = jnp.square(h_ref[...].astype(f32)).astype(bf16)
+    load_g = pltpu.make_async_copy(basis_g_ref, basis_g, basis_sem.at[0])
+    load_h = pltpu.make_async_copy(basis_h_ref, basis_h, basis_sem.at[1])
+    load_g.start()
+    load_h.start()
+
+    def each(first, last, act):
+        def once(d, _):
+            act(d)
+            return 0
+
+        lax.fori_loop(first, last, once, 0)
+
+    tokens = grad_ref.shape[0]
+    top = routes_ref.shape[1]
+    sent = tokens * top
+    named = jnp.concatenate([routes_ref[:, j : j + 1] for j in range(top)], axis=0)
+    onehot = (named == lax.broadcasted_iota(jnp.int32, (sent, 128), 1)).astype(f32).astype(bf16)
+
+    def order_of(axis):
+        index = lax.broadcasted_iota(jnp.int32, (sent, sent), axis)
+        return jnp.where(index < tokens, index * top, (index - tokens) * top + 1)
+
+    lower = (order_of(1) < order_of(0)).astype(f32).astype(bf16)
+    before = jnp.dot(lower, onehot, preferred_element_type=f32)
+    within = jnp.sum(before * onehot.astype(f32), axis=1, keepdims=True).astype(jnp.int32)
+    slots = named * capacity + within
+    chosen = (slots == lax.broadcasted_iota(jnp.int32, (sent, experts * capacity), 1)).astype(f32)
+    picked = chosen.T.astype(bf16)
+    token_grad = grad_ref[...].astype(f32)
+    weighted = jnp.concatenate(
+        [(weight_ref[:, j : j + 1] * token_grad).astype(bf16) for j in range(top)], axis=0
+    )
+    send_g[...] = (
+        jnp.dot(picked, weighted, preferred_element_type=f32).astype(bf16).reshape(send_g.shape)
+    )
+
+    def dispatch_copy(source, target, ssem, rsem, d):
+        to = lax.rem(e + d, experts)
+        return pltpu.make_async_remote_copy(
+            source.at[to],
+            target.at[d],
+            ssem.at[d],
+            rsem.at[d],
+            device_id={"expert": to},
+            device_id_type=MESH,
+        )
+
+    def dg_copy(d):
+        return dispatch_copy(send_g, held_g, dg_s, dg_r, d)
+
+    def dh_copy(d):
+        return dispatch_copy(send_h, held_h, dh_s, dh_r, d)
+
+    pl.semaphore_wait(barrier, 2 * chips - 1 + experts - 1)
+    each(1, experts, lambda d: dg_copy(d).start())
+    send_h[...] = (
+        jnp.dot(picked, hidden_ref[...], preferred_element_type=f32)
+        .astype(bf16)
+        .reshape(send_h.shape)
+    )
+    each(1, experts, lambda d: dh_copy(d).start())
     acc[...] = jnp.zeros_like(acc)
-    pl.semaphore_wait(barrier, 2 * chips - 1 + experts - 1)
+
+    def rotate(value, basis, rotated, squared, first):
+        turned = jnp.dot(value, basis[...], preferred_element_type=f32).astype(bf16)
+        count = value.shape[0]
+        rotated[first : first + count, :] = turned
+        squared[first : first + count, :] = jnp.square(turned.astype(f32)).astype(bf16)
+
+    load_h.wait()
+    load_g.wait()
+    rotate(send_g[e], basis_g, g_ref, gsq, 0)
+    query_row = lax.broadcasted_iota(jnp.int32, (query_g_ref.shape[0], 1), 0) == ids_ref[0, 0]
+
+    def query(ref, basis):
+        turned = jnp.dot(ref[...], basis[...], preferred_element_type=f32)
+        one = jnp.sum(jnp.where(query_row, turned, 0.0), axis=0, keepdims=True)
+        return one.astype(bf16).astype(f32)
+
+    query_g = query(query_g_ref, basis_g)
+    query_h = query(query_h_ref, basis_h)
+    for first, last in ((1, experts // 2), (experts // 2, experts)):
+        each(first, last, lambda d: dg_copy(d).wait_recv())
+        rotate(
+            held_g[first:last].reshape((last - first) * capacity, width_d),
+            basis_g,
+            g_ref,
+            gsq,
+            first * capacity,
+        )
+    each(1, experts, lambda d: dh_copy(d).wait_recv())
+    rotate(
+        jnp.concatenate(
+            [send_h[e], held_h[1:experts].reshape((experts - 1) * capacity, width_ff)], axis=0
+        ),
+        basis_h,
+        h_ref,
+        hsq,
+        0,
+    )
 
     def core_copy(c):
         return pltpu.make_async_remote_copy(
@@ -157,13 +270,6 @@
             device_id=dp_id(lax.rem(me + d, 2 * chips)),
             device_id_type=MESH,
         )
-
-    def each(first, last, act):
-        def once(d, _):
-            act(d)
-            return 0
-
-        lax.fori_loop(first, last, once, 0)
 
     for pair in range(chunks // 2):
         both = lax.dot_general(
@@ -183,8 +289,11 @@
     row_g = jnp.sum(gsq[...].astype(f32), axis=1, keepdims=True)
     row_h = jnp.sum(hsq[...].astype(f32), axis=1, keepdims=True)
     own_sum = jnp.sum(row_g * row_h, axis=0, keepdims=True)
-    place = lax.broadcasted_iota(jnp.int32, small_ref.shape, 0)
-    small[me] = jnp.where(place == 22, jnp.broadcast_to(own_sum, small_ref.shape), small_ref[...])
+    for j in range(width_d // 128):
+        small[me, j : j + 1, :] = query_g[:, j * 128 : (j + 1) * 128]
+    for j in range(width_ff // 128):
+        small[me, 16 + j : 17 + j, :] = query_h[:, j * 128 : (j + 1) * 128]
+    small[me, 22:24, :] = jnp.broadcast_to(own_sum, (2, 128))
     each(1, 2 * chips, lambda d: small_copy(d, me).start())
 
     def stage_one(c):
@@ -295,23 +404,18 @@
     ret_out[...] = (acc[...] / root).reshape(ret_out.shape)
 
     def ret_copy(d, slot):
-        to = lax.rem(e + d, experts)
-        return pltpu.make_async_remote_copy(
-            ret_out.at[to],
+        return pltpu.make_async_remote_copy(
+            ret_out.at[d],
             ret_in.at[slot],
             ret_s.at[d],
             ret_r.at[d],
-            device_id={"expert": to},
+            device_id={"expert": lax.rem(e + experts - d, experts)},
             device_id_type=MESH,
         )
 
     each(1, experts, lambda d: ret_copy(d, e).start())
-    ret_in[e] = ret_out[e]
-    chosen = (
-        slots_ref[...]
-        == lax.broadcasted_iota(jnp.int32, (out_ref.shape[0], experts * capacity), 1)
-    ).astype(f32)
-    each(1, experts, lambda d: ret_copy(d, lax.rem(e + experts - d, experts)).wait_recv())
+    ret_in[e] = ret_out[0]
+    each(1, experts, lambda d: ret_copy(d, lax.rem(e + d, experts)).wait_recv())
     out_ref[...] = jnp.dot(
         chosen,
         ret_in[...].reshape(experts * capacity, -1),
@@ -324,31 +428,58 @@
         cg_copy(c, k).wait_send()
     each(1, 2 * chips, lambda d: small_copy(d, me).wait_send())
     each(1, experts, lambda d: ret_copy(d, e).wait_send())
-
-
-def back_half(grad, hid, small, slots, damp, experts, capacity, replicas):
-    rows, width_d = grad.shape
-    width_ff = hid.shape[1]
+    each(1, experts, lambda d: dg_copy(d).wait_send())
+    each(1, experts, lambda d: dh_copy(d).wait_send())
+
+
+def body(
+    token_hidden,
+    token_grad,
+    routes,
+    route_weight,
+    gradient_eigenbasis,
+    basis_hidden,
+    query_hidden,
+    query_grad,
+    query_ids,
+    damping,
+):
+    experts = lax.axis_size("expert")
+    replicas = lax.axis_size(DP)
+    tokens, top, width_ff = token_hidden.shape
+    width_d = token_grad.shape[1]
+    capacity = tokens * top * 3 // (2 * experts)
+    rows = experts * capacity
     chips = replicas // 2
     chunks = width_ff // CHUNK
     bf16, f32 = jnp.bfloat16, jnp.float32
     block = width_d // replicas
     dma = pltpu.SemaphoreType.DMA
     vmem = pl.BlockSpec(memory_space=pltpu.VMEM)
-    return pl.pallas_call(
+    anywhere = pl.BlockSpec(memory_space=pl.ANY)
+    smem = pl.BlockSpec(memory_space=pltpu.SMEM)
+    picked, corrections = pl.pallas_call(
         functools.partial(
             back_kernel, 1.0 / (replicas * experts * capacity), math.sqrt(width_d * width_ff)
         ),
         out_shape=(
-            jax.ShapeDtypeStruct((slots.shape[0], 128), f32),
+            jax.ShapeDtypeStruct((tokens * top, 128), f32),
             jax.ShapeDtypeStruct((block, width_ff), f32),
         ),
-        in_specs=[vmem] * 5,
+        in_specs=[vmem] * 4 + [anywhere] * 2 + [vmem] * 2 + [smem, vmem],
         out_specs=(vmem, vmem),
         scratch_shapes=[
+            pltpu.VMEM((width_d, width_d), bf16),
+            pltpu.VMEM((width_ff, width_ff), bf16),
+            pltpu.VMEM((experts, capacity, width_d), bf16),
+            pltpu.VMEM((experts, capacity, width_ff), bf16),
+            pltpu.VMEM((experts, capacity, width_d), bf16),
+            pltpu.VMEM((experts, capacity, width_ff), bf16),
             pltpu.VMEM((rows, width_d), bf16),
             pltpu.VMEM((rows, width_ff), bf16),
-            pltpu.VMEM((replicas, *small.shape), f32),
+            pltpu.VMEM((rows, width_d), bf16),
+            pltpu.VMEM((rows, width_ff), bf16),
+            pltpu.VMEM((replicas, 24, 128), f32),
             pltpu.VMEM((chunks, 2, chips, CHUNK, block), bf16),
             pltpu.VMEM((chunks, chips, CHUNK, block), bf16),
             pltpu.VMEM((chunks, chips, CHUNK, block), bf16),
@@ -357,6 +488,11 @@
             pltpu.VMEM((rows, 128), f32),
             pltpu.VMEM((experts, capacity, 128), f32),
             pltpu.VMEM((experts, capacity, 128), f32),
+            dma((2,)),
+            dma((experts,)),
+            dma((experts,)),
+            dma((experts,)),
+            dma((experts,)),
             dma((replicas,)),
             dma((replicas,)),
             dma((chunks,)),
@@ -373,76 +509,19 @@
         compiler_params=pltpu.CompilerParams(
             collective_id=0, has_side_effects=True, vmem_limit_bytes=60 * 1024 * 1024
         ),
-    )(grad, hid, small, slots, damp)
-
-
-def slot_index(routes_flat, experts, capacity):
-    onehot = (routes_flat[:, None] == jnp.arange(experts, dtype=jnp.int32)[None, :]).astype(
-        jnp.int32
-    )
-    before = jnp.cumsum(onehot, axis=0) - onehot
-    return routes_flat * capacity + jnp.sum(before * onehot, axis=1)
-
-
-def traded(blocks, axis):
-    return lax.all_to_all(blocks, axis, split_axis=0, concat_axis=0, tiled=True)
-
-
-def body(
-    token_hidden,
-    token_grad,
-    routes,
-    route_weight,
-    gradient_eigenbasis,
-    basis_hidden,
-    query_hidden,
-    query_grad,
-    query_ids,
-    damping,
-):
-    experts = lax.axis_size("expert")
-    replicas = lax.axis_size(DP)
-    tok_rows, top, width_ff = token_hidden.shape
-    width_d = token_grad.shape[1]
-    capacity = tok_rows * top * 3 // (2 * experts)
-    slots = slot_index(routes.reshape(-1), experts, capacity)
-    weighted = (route_weight[:, :, None] * token_grad[:, None, :].astype(jnp.float32)).astype(
-        jnp.bfloat16
-    )
-    rows = jnp.concatenate(
-        (token_hidden.reshape(-1, width_ff), weighted.reshape(-1, width_d)), axis=1
-    )
-    chosen = (slots[None, :] == jnp.arange(experts * capacity, dtype=jnp.int32)[:, None]).astype(
-        jnp.bfloat16
-    )
-    sent = jnp.dot(chosen, rows, preferred_element_type=jnp.float32).astype(jnp.bfloat16)
-    held = traded(sent.reshape(experts, capacity, -1), "expert").reshape(experts * capacity, -1)
-    rotate_h = basis_hidden[0]
-    rotate_gradient = gradient_eigenbasis[0]
-    picks = query_ids[0]
-    query_g = jnp.take(query_grad[0], picks, axis=0)
-    query_h = jnp.take(query_hidden[0], picks, axis=0)
-    query_g_rot = jnp.dot(query_g, rotate_gradient, preferred_element_type=jnp.float32)
-    query_h_rot = jnp.dot(query_h, rotate_h, preferred_element_type=jnp.float32)
-    hid = jnp.dot(held[:, :width_ff], rotate_h, preferred_element_type=jnp.float32).astype(
-        jnp.bfloat16
-    )
-    grad = jnp.dot(held[:, width_ff:], rotate_gradient, preferred_element_type=jnp.float32).astype(
-        jnp.bfloat16
-    )
-    small = jnp.concatenate(
-        (
-            query_g_rot.astype(jnp.bfloat16).astype(jnp.float32).reshape(-1, 128),
-            query_h_rot.astype(jnp.bfloat16).astype(jnp.float32).reshape(-1, 128),
-            jnp.zeros((2, 128), jnp.float32),
-        ),
-        axis=0,
-    )
-    damp = jnp.broadcast_to(damping[:, None], (1, 128))
-    picked, corrections = back_half(
-        grad, hid, small, slots[:, None], damp, experts, capacity, replicas
-    )
-    scores = picked[:, :replicas].reshape(tok_rows, top, replicas)
+    )(
+        routes,
+        route_weight,
+        token_hidden.swapaxes(0, 1).reshape(tokens * top, width_ff),
+        token_grad,
+        gradient_eigenbasis[0],
+        basis_hidden[0],
+        query_grad[0],
+        query_hidden[0],
+        query_ids,
+        jnp.broadcast_to(damping[:, None], (1, 128)),
+    )
+    scores = picked[:, :replicas].reshape(top, tokens, replicas).swapaxes(0, 1)
     return (scores, corrections[None])
 
 

time: 138 us -> 119 us (0.86)
  Pallas kernels: 70.8 us -> 109 us
  waiting for transfers between devices: 23.4 us -> 0 us
  matrix products: 17.2 us -> 0 us
  starting transfers between devices: 8.03 us -> 0 us
  local copies, waits for them, and re-layouts: 12.5 us -> 8.53 us
  other arithmetic: 3.19 us -> 0 us
    pallas_call x1, Pallas kernels: 70.8 us -> 109 us  [body(): pl.pallas_call(functools.partial(back_kernel, 1.0 / (replicas * experts *...]
    all_to_all x1 -> x0, waiting for transfers between devices: 23.4 us -> none  [traded(): return lax.all_to_all(blocks, axis, split_axis=0, concat_axis=0, tiled=True)]
    dot_general x5 -> x0, matrix products: 17.2 us -> none  [the longest x1 8.03 us: body(): jnp.dot(held[:, width_ff:], rotate_gradient, preferred_element_type=jnp.f...]
    all_to_all x1 -> x0, starting transfers between devices: 8.03 us -> none  [traded(): return lax.all_to_all(blocks, axis, split_axis=0, concat_axis=0, tiled=True)]
    mul x5 -> x0, local copies, waits for them, and re-layouts: 4.98 us -> none  [the longest x3 4.73 us: body(): route_weight[:, :, None] * token_grad[:, None, :].astype(jnp.float32)]
    transpose x0 -> x1, local copies, waits for them, and re-layouts: none -> 1.78 us  [body(): token_hidden.swapaxes(0, 1).reshape(tokens * top, width_ff)]
    convert_element_type x2 -> x0, other arithmetic: 1.77 us -> none  [the longest x1 1.77 us: body(): (route_weight[:, :, None] * token_grad[:, None, :].astype(jnp.float32)).a...]
    unnamed x10 -> x3, local copies, waits for them, and re-layouts: 4.36 us -> 4.6 us
  transfers between devices with their start and end apart: 1 -> 0, of which waited for: 1 -> 0; matrix products, arithmetic and copies ran while one was open for 5% -> 0% of each run, Pallas kernels for 0% -> 0%
where the time goes in v3:
time: 119 us
  Pallas kernels  109 us (92%)
  local copies, waits for them, and re-layouts  8.53 us (7%)
  between operations  1.93 us (2%)
    pallas_call x1, Pallas kernels, body(): pl.pallas_call(functools.partial(back_kernel, 1.0 / (replicas * experts *...  109 us
    unnamed x3, local copies, waits for them, and re-layouts  4.6 us

profile of v3, /device:TPU:0, one launch (start us, length us, event | category | flops | bytes accessed | tf_op | source)
XLA Modules:
  0.0 119.0 jit_solution(12245587151326809252)
XLA Ops:
  1.9 0.6 broadcast_in_dim.12.damp_ref
  2.5 1.4 %copy.13.routes_ref = s32[128,2]{1,0:T(8,128)} copy(s32[128,2]{0,1:T(2,128)} %param.12) | data formatting | bytes 2048 | tf_op args[2]
  3.9 1.4 %copy.14.weight_ref = f32[128,2]{1,0:T(8,128)} copy(f32[128,2]{0,1:T(2,128)} %param.13) | data formatting | bytes 2048 | tf_op args[3]
  5.3 1.8 %copy.12 = bf16[2,128,768]{2,1,0:T(8,128)(2,1)} copy(bf16[2,128,768]{2,0,1:T(2,128)(2,1)} %bitcast.15) | data formatting | bytes 786432 | tf_op jit(solution)/shard_map/transpose | solution.py:515
  7.1 108.5 %shard_map.113 = (f32[256,128]{1,0:T(8,128)}, f32[128,768]{1,0:T(8,128)}) custom-call(s32[128,2]{1,0:T(8,128)} %copy.13.routes_ref, f32[128,2]{1,0:T(8,128)} %copy.14.weight_ref, bf16[256,768]{1,0:T(8,128)(2,1)} %bitcast.13, bf16[128,2048]{1,0:T(8,128)(2,1)} %grad_ref.1, bf16[2048,2048]{1,0:T(8,128)(2,1)} %bitcast.12, bf16[768,768]{1,0:T(8,128)(2,1)} %bitcast.14, ...), custom_call_target="tpu_custom_call" | custom-call | tf_op jit(solution)/shard_map/pallas_call | solution.py:461
  115.6 1.6 %copy.15 = f32[2,128,16]{1,2,0:T(8,128)} copy(f32[2,128,16]{2,1,0:T(8,128)} %bitcast.17) | data formatting | bytes 32768 | tf_op jit(solution)/shard_map/reshape | solution.py:524
  117.2 1.8 %copy.19 = f32[1,128,768]{2,1,0:T(8,128)} copy(f32[1,128,768]{2,1,0:T(8,128)} %bitcast.16) | data formatting | bytes 786432

commit v4 on v3

--- a/solution.py
+++ b/solution.py
@@ -17,6 +17,12 @@
 
 MESH = pl.DeviceIdType.MESH
 CHUNK = 128
+ORDER = (
+    ("C", 0), ("A", 2), ("C", 1), ("A", 3), ("E", 0), ("C", 2), ("A", 4), ("E", 1), ("C", 3),
+    ("A", 5), ("R", 0), ("R", 1), ("S", 0, 0, 1), ("E", 2), ("C", 4), ("S", 0, 1, 3), ("E", 3),
+    ("C", 5), ("S", 0, 3, 4), ("R", 2), ("R", 3), ("S", 1, 0, 2), ("E", 4), ("S", 1, 2, 4),
+    ("E", 5), ("R", 4), ("R", 5), ("S", 2, 0, 4),
+)
 
 
 def back_kernel(
@@ -120,28 +126,25 @@
         lax.fori_loop(first, last, once, 0)
 
     tokens = grad_ref.shape[0]
-    top = routes_ref.shape[1]
+    top = routes_ref.shape[0]
     sent = tokens * top
-    named = jnp.concatenate([routes_ref[:, j : j + 1] for j in range(top)], axis=0)
-    onehot = (named == lax.broadcasted_iota(jnp.int32, (sent, 128), 1)).astype(f32).astype(bf16)
+    named = jnp.concatenate([routes_ref[j : j + 1, :] for j in range(top)], axis=1)
+    onehot = (named == lax.broadcasted_iota(jnp.int32, (16, sent), 0)).astype(f32)
 
     def order_of(axis):
         index = lax.broadcasted_iota(jnp.int32, (sent, sent), axis)
         return jnp.where(index < tokens, index * top, (index - tokens) * top + 1)
 
-    lower = (order_of(1) < order_of(0)).astype(f32).astype(bf16)
-    before = jnp.dot(lower, onehot, preferred_element_type=f32)
-    within = jnp.sum(before * onehot.astype(f32), axis=1, keepdims=True).astype(jnp.int32)
+    earlier = (order_of(0) < order_of(1)).astype(f32).astype(bf16)
+    before = jnp.dot(onehot.astype(bf16), earlier, preferred_element_type=f32)
+    within = jnp.sum(before * onehot, axis=0, keepdims=True).astype(jnp.int32)
     slots = named * capacity + within
-    chosen = (slots == lax.broadcasted_iota(jnp.int32, (sent, experts * capacity), 1)).astype(f32)
-    picked = chosen.T.astype(bf16)
-    token_grad = grad_ref[...].astype(f32)
-    weighted = jnp.concatenate(
-        [(weight_ref[:, j : j + 1] * token_grad).astype(bf16) for j in range(top)], axis=0
-    )
-    send_g[...] = (
-        jnp.dot(picked, weighted, preferred_element_type=f32).astype(bf16).reshape(send_g.shape)
-    )
+    chosen = (slots == lax.broadcasted_iota(jnp.int32, (experts * capacity, sent), 0)).astype(f32)
+    weights = jnp.concatenate([weight_ref[j : j + 1, :] for j in range(top)], axis=1)
+    weight = jnp.sum(chosen * weights, axis=1, keepdims=True)
+    picks = [chosen[:, j * tokens : (j + 1) * tokens].astype(bf16) for j in range(top)]
+    gathered = jnp.dot(sum(picks[1:], picks[0]), grad_ref[...], preferred_element_type=f32)
+    send_g[...] = (weight * gathered).astype(bf16).reshape(send_g.shape)
 
     def dispatch_copy(source, target, ssem, rsem, d):
         to = lax.rem(e + d, experts)
@@ -162,11 +165,12 @@
 
     pl.semaphore_wait(barrier, 2 * chips - 1 + experts - 1)
     each(1, experts, lambda d: dg_copy(d).start())
-    send_h[...] = (
-        jnp.dot(picked, hidden_ref[...], preferred_element_type=f32)
-        .astype(bf16)
-        .reshape(send_h.shape)
-    )
+    hidden = hidden_ref[...].astype(f32)
+    moved = None
+    for j in range(top):
+        part_j = jnp.dot(picks[j], hidden[:, j, :].astype(bf16), preferred_element_type=f32)
+        moved = part_j if moved is None else moved + part_j
+    send_h[...] = moved.astype(bf16).reshape(send_h.shape)
     each(1, experts, lambda d: dh_copy(d).start())
     acc[...] = jnp.zeros_like(acc)
 
@@ -174,11 +178,13 @@
         turned = jnp.dot(value, basis[...], preferred_element_type=f32).astype(bf16)
         count = value.shape[0]
         rotated[first : first + count, :] = turned
-        squared[first : first + count, :] = jnp.square(turned.astype(f32)).astype(bf16)
+        square = jnp.square(turned.astype(f32)).astype(bf16)
+        squared[first : first + count, :] = square
+        return jnp.sum(square.astype(f32), axis=1, keepdims=True)
 
     load_h.wait()
     load_g.wait()
-    rotate(send_g[e], basis_g, g_ref, gsq, 0)
+    row_g = [rotate(send_g[e], basis_g, g_ref, gsq, 0)]
     query_row = lax.broadcasted_iota(jnp.int32, (query_g_ref.shape[0], 1), 0) == ids_ref[0, 0]
 
     def query(ref, basis):
@@ -190,15 +196,17 @@
     query_h = query(query_h_ref, basis_h)
     for first, last in ((1, experts // 2), (experts // 2, experts)):
         each(first, last, lambda d: dg_copy(d).wait_recv())
-        rotate(
-            held_g[first:last].reshape((last - first) * capacity, width_d),
-            basis_g,
-            g_ref,
-            gsq,
-            first * capacity,
+        row_g.append(
+            rotate(
+                held_g[first:last].reshape((last - first) * capacity, width_d),
+                basis_g,
+                g_ref,
+                gsq,
+                first * capacity,
+            )
         )
     each(1, experts, lambda d: dh_copy(d).wait_recv())
-    rotate(
+    row_h = rotate(
         jnp.concatenate(
             [send_h[e], held_h[1:experts].reshape((experts - 1) * capacity, width_ff)], axis=0
         ),
@@ -271,7 +279,7 @@
             device_id_type=MESH,
         )
 
-    for pair in range(chunks // 2):
+    def spread(pair):
         both = lax.dot_general(
             hsq[:, pair * 2 * CHUNK : (pair + 1) * 2 * CHUNK],
             gsq[...],
@@ -283,18 +291,16 @@
                 part[2 * pair + half, q % 2, q // 2] = both[
                     half * CHUNK : (half + 1) * CHUNK, q * CHUNK : (q + 1) * CHUNK
                 ]
-        for half in range(2):
             core_copy(2 * pair + half).start()
 
-    row_g = jnp.sum(gsq[...].astype(f32), axis=1, keepdims=True)
-    row_h = jnp.sum(hsq[...].astype(f32), axis=1, keepdims=True)
-    own_sum = jnp.sum(row_g * row_h, axis=0, keepdims=True)
-    for j in range(width_d // 128):
-        small[me, j : j + 1, :] = query_g[:, j * 128 : (j + 1) * 128]
-    for j in range(width_ff // 128):
-        small[me, 16 + j : 17 + j, :] = query_h[:, j * 128 : (j + 1) * 128]
-    small[me, 22:24, :] = jnp.broadcast_to(own_sum, (2, 128))
-    each(1, 2 * chips, lambda d: small_copy(d, me).start())
+    def share():
+        own_sum = jnp.sum(jnp.concatenate(row_g, axis=0) * row_h, axis=0, keepdims=True)
+        for j in range(width_d // 128):
+            small[me, j : j + 1, :] = query_g[:, j * 128 : (j + 1) * 128]
+        for j in range(width_ff // 128):
+            small[me, 16 + j : 17 + j, :] = query_h[:, j * 128 : (j + 1) * 128]
+        small[me, 22:24, :] = jnp.broadcast_to(own_sum, (2, 128))
+        each(1, 2 * chips, lambda d: small_copy(d, me).start())
 
     def stage_one(c):
         core_copy(c).wait()
@@ -360,46 +366,27 @@
 
         lax.fori_loop(first, last, step, 0)
 
+    def small_arrival(d):
+        small_copy(d, lax.rem(me + 2 * chips - d, 2 * chips)).wait_recv()
+
+    spread(0)
+    share()
+    spread(1)
     stage_one(0)
     stage_one(1)
-
-    def small_arrival(d):
-        small_copy(d, lax.rem(me + 2 * chips - d, 2 * chips)).wait_recv()
-
+    spread(2)
     each(1, 2 * chips, small_arrival)
     complete = small[0, 22:23, :]
     for n in range(1, 2 * chips):
         complete = complete + small[n, 22:23, :]
-    level = damp_ref[...] * (complete * (scale / (width_d * width_ff)) + eps)
-
-    stage_two(0, level)
-    stage_one(2)
-    stage_two(1, level)
-    stage_one(3)
-    stage_three(0)
-    stage_two(2, level)
-    stage_one(4)
-    stage_three(1)
-    stage_two(3, level)
-    stage_one(5)
-    ready(0)
-    ready(1)
-    score(0, 0, 2)
-    stage_three(2)
-    score(0, 2, 3)
-    stage_two(4, level)
-    score(0, 3, 4)
-    stage_three(3)
-    stage_two(5, level)
-    ready(2)
-    ready(3)
-    score(1, 0, 2)
-    stage_three(4)
-    score(1, 2, 4)
-    stage_three(5)
-    ready(4)
-    ready(5)
-    score(2, 0, 4)
+    level = damp_ref[0] * (complete * (scale / (width_d * width_ff)) + eps)
+
+    stages = {"A": stage_one, "C": lambda c: stage_two(c, level), "E": stage_three, "R": ready}
+    for act, c, *span in ORDER:
+        if act == "S":
+            score(c, *span)
+        else:
+            stages[act](c)
 
     ret_out[...] = (acc[...] / root).reshape(ret_out.shape)
 
@@ -416,12 +403,15 @@
     each(1, experts, lambda d: ret_copy(d, e).start())
     ret_in[e] = ret_out[0]
     each(1, experts, lambda d: ret_copy(d, lax.rem(e + d, experts)).wait_recv())
-    out_ref[...] = jnp.dot(
+    result = lax.dot_general(
+        ret_in[...].reshape(experts * capacity, -1),
         chosen,
-        ret_in[...].reshape(experts * capacity, -1),
+        (((0,), (0,)), ((), ())),
         preferred_element_type=f32,
         precision=lax.Precision.HIGHEST,
     )
+    for j in range(top):
+        out_ref[j] = result[: out_ref.shape[1], j * tokens : (j + 1) * tokens]
     for c in range(chunks):
         each(1, chips, lambda d: rs_copy(c, d).wait_send())
         each(1, chips, lambda d: ag_copy(c, d).wait_send())
@@ -463,10 +453,10 @@
             back_kernel, 1.0 / (replicas * experts * capacity), math.sqrt(width_d * width_ff)
         ),
         out_shape=(
-            jax.ShapeDtypeStruct((tokens * top, 128), f32),
+            jax.ShapeDtypeStruct((top, replicas, tokens), f32),
             jax.ShapeDtypeStruct((block, width_ff), f32),
         ),
-        in_specs=[vmem] * 4 + [anywhere] * 2 + [vmem] * 2 + [smem, vmem],
+        in_specs=[vmem] * 4 + [anywhere] * 2 + [vmem] * 2 + [smem] * 2,
         out_specs=(vmem, vmem),
         scratch_shapes=[
             pltpu.VMEM((width_d, width_d), bf16),
@@ -510,19 +500,18 @@
             collective_id=0, has_side_effects=True, vmem_limit_bytes=60 * 1024 * 1024
         ),
     )(
-        routes,
-        route_weight,
-        token_hidden.swapaxes(0, 1).reshape(tokens * top, width_ff),
+        routes.T,
+        route_weight.T,
+        token_hidden,
         token_grad,
         gradient_eigenbasis[0],
         basis_hidden[0],
         query_grad[0],
         query_hidden[0],
         query_ids,
-        jnp.broadcast_to(damping[:, None], (1, 128)),
+        damping,
     )
-    scores = picked[:, :replicas].reshape(top, tokens, replicas).swapaxes(0, 1)
-    return (scores, corrections[None])
+    return (picked.transpose(2, 0, 1), corrections[None])
 
 
 def solution(mesh):

time: 119 us -> 111 us (0.933); the launches traced: 119 us -> 109 us
  local copies, waits for them, and re-layouts: 8.53 us -> 3.09 us
  Pallas kernels: 109 us -> 104 us
    pallas_call x1, Pallas kernels: 109 us -> 104 us  [body(): pl.pallas_call(functools.partial(back_kernel, 1.0 / (replicas * experts *...]
    transpose x1 -> x0, local copies, waits for them, and re-layouts: 1.78 us -> none  [body(): token_hidden.swapaxes(0, 1).reshape(tokens * top, width_ff)]
    reshape x1 -> x0, local copies, waits for them, and re-layouts: 1.58 us -> none  [body(): scores = picked[:, :replicas].reshape(top, tokens, replicas).swapaxes(0, 1)]
    unnamed x3 -> x2, local copies, waits for them, and re-layouts: 4.6 us -> 3.09 us
where the time goes in v4:
time: 111 us; the launch traced here: 109 us
  Pallas kernels  104 us (94%)
  local copies, waits for them, and re-layouts  3.09 us (3%)
  between operations  1.93 us (2%)
    pallas_call x1, Pallas kernels, body(): pl.pallas_call(functools.partial(back_kernel, 1.0 / (replicas * experts *...  104 us
    unnamed x2, local copies, waits for them, and re-layouts  3.09 us

profile of v4, /device:TPU:0, one launch (start us, length us, event | category | flops | bytes accessed | tf_op | source)
XLA Modules:
  0.0 108.7 jit_solution(14408627428051508998)
XLA Ops:
  1.9 103.7 %shard_map.113 = (f32[2,16,128]{2,1,0:T(8,128)}, f32[128,768]{1,0:T(8,128)}) custom-call(s32[2,128]{1,0:T(2,128)} %bitcast.14, f32[2,128]{1,0:T(2,128)} %bitcast.15, bf16[128,2,768]{2,1,0:T(2,128)(2,1)} %hidden_ref.1, bf16[128,2048]{1,0:T(8,128)(2,1)} %grad_ref.1, bf16[2048,2048]{1,0:T(8,128)(2,1)} %bitcast.8, bf16[768,768]{1,0:T(8,128)(2,1)} %bitcast.9, ...), custom_call_target="tpu_custom_call" | custom-call | tf_op jit(solution)/shard_map/pallas_call | solution.py:451
  105.6 1.3 %copy.16 = f32[128,2,16]{0,2,1:T(8,128)} copy(f32[128,2,16]{0,2,1:T(8,128)} %bitcast.12) | data formatting | bytes 32768
  106.9 1.8 %copy.17 = f32[1,128,768]{2,1,0:T(8,128)} copy(f32[1,128,768]{2,1,0:T(8,128)} %bitcast.10) | data formatting | bytes 786432

commit v5 on v4

--- a/solution.py
+++ b/solution.py
@@ -18,10 +18,10 @@
 MESH = pl.DeviceIdType.MESH
 CHUNK = 128
 ORDER = (
-    ("C", 0), ("A", 2), ("C", 1), ("A", 3), ("E", 0), ("C", 2), ("A", 4), ("E", 1), ("C", 3),
-    ("A", 5), ("R", 0), ("R", 1), ("S", 0, 0, 1), ("E", 2), ("C", 4), ("S", 0, 1, 3), ("E", 3),
-    ("C", 5), ("S", 0, 3, 4), ("R", 2), ("R", 3), ("S", 1, 0, 2), ("E", 4), ("S", 1, 2, 4),
-    ("E", 5), ("R", 4), ("R", 5), ("S", 2, 0, 4),
+    ("C", 0), ("A", 2), ("C", 1), ("A", 3), ("E", 0), ("C", 2), ("A", 4), ("E", 1), ("R", 0),
+    ("R", 1), ("S", 0, 0, 1), ("C", 3), ("A", 5), ("S", 0, 1, 2), ("E", 2), ("S", 0, 2, 4),
+    ("C", 4), ("E", 3), ("R", 2), ("R", 3), ("S", 1, 0, 1), ("C", 5), ("S", 1, 1, 3), ("E", 4),
+    ("S", 1, 3, 4), ("E", 5), ("R", 4), ("R", 5), ("S", 2, 0, 4),
 )
 
 
@@ -42,6 +42,10 @@
     corr_ref,
     basis_g,
     basis_h,
+    token_hidden,
+    token_grad,
+    query_rows_g,
+    query_rows_h,
     send_g,
     send_h,
     held_g,
@@ -51,6 +55,8 @@
     gsq,
     hsq,
     small,
+    sums,
+    back,
     part,
     nearby,
     summed,
@@ -66,6 +72,8 @@
     dh_r,
     small_s,
     small_r,
+    ask_s,
+    ask_r,
     core_s,
     core_r,
     rs_s,
@@ -84,7 +92,7 @@
     xz = x * 2 + z
     chips = part.shape[2]
     experts = ret_out.shape[0]
-    capacity = ret_out.shape[1]
+    capacity = held_g.shape[1]
     rows, width_d = g_ref.shape
     width_ff = h_ref.shape[1]
     chunks = width_ff // CHUNK
@@ -113,10 +121,21 @@
 
     lax.fori_loop(1, 2 * chips, greet_dp, 0)
     lax.fori_loop(1, experts, greet_expert, 0)
-    load_g = pltpu.make_async_copy(basis_g_ref, basis_g, basis_sem.at[0])
-    load_h = pltpu.make_async_copy(basis_h_ref, basis_h, basis_sem.at[1])
-    load_g.start()
-    load_h.start()
+    loads = [
+        pltpu.make_async_copy(source, target, basis_sem.at[index])
+        for index, (source, target) in enumerate(
+            (
+                (grad_ref, token_grad),
+                (hidden_ref, token_hidden),
+                (query_g_ref, query_rows_g),
+                (query_h_ref, query_rows_h),
+                (basis_h_ref, basis_h),
+                (basis_g_ref, basis_g),
+            )
+        )
+    ]
+    for load in loads:
+        load.start()
 
     def each(first, last, act):
         def once(d, _):
@@ -143,7 +162,8 @@
     weights = jnp.concatenate([weight_ref[j : j + 1, :] for j in range(top)], axis=1)
     weight = jnp.sum(chosen * weights, axis=1, keepdims=True)
     picks = [chosen[:, j * tokens : (j + 1) * tokens].astype(bf16) for j in range(top)]
-    gathered = jnp.dot(sum(picks[1:], picks[0]), grad_ref[...], preferred_element_type=f32)
+    loads[0].wait()
+    gathered = jnp.dot(sum(picks[1:], picks[0]), token_grad[...], preferred_element_type=f32)
     send_g[...] = (weight * gathered).astype(bf16).reshape(send_g.shape)
 
     def dispatch_copy(source, target, ssem, rsem, d):
@@ -165,7 +185,8 @@
 
     pl.semaphore_wait(barrier, 2 * chips - 1 + experts - 1)
     each(1, experts, lambda d: dg_copy(d).start())
-    hidden = hidden_ref[...].astype(f32)
+    loads[1].wait()
+    hidden = token_hidden[...].astype(f32)
     moved = None
     for j in range(top):
         part_j = jnp.dot(picks[j], hidden[:, j, :].astype(bf16), preferred_element_type=f32)
@@ -173,6 +194,9 @@
     send_h[...] = moved.astype(bf16).reshape(send_h.shape)
     each(1, experts, lambda d: dh_copy(d).start())
     acc[...] = jnp.zeros_like(acc)
+    back[...] = jnp.zeros_like(back)
+    for j in range(experts):
+        back[j, :capacity, :] = chosen[j * capacity : (j + 1) * capacity].astype(bf16)
 
     def rotate(value, basis, rotated, squared, first):
         turned = jnp.dot(value, basis[...], preferred_element_type=f32).astype(bf16)
@@ -182,8 +206,8 @@
         squared[first : first + count, :] = square
         return jnp.sum(square.astype(f32), axis=1, keepdims=True)
 
-    load_h.wait()
-    load_g.wait()
+    for load in loads[2:]:
+        load.wait()
     row_g = [rotate(send_g[e], basis_g, g_ref, gsq, 0)]
     query_row = lax.broadcasted_iota(jnp.int32, (query_g_ref.shape[0], 1), 0) == ids_ref[0, 0]
 
@@ -192,8 +216,44 @@
         one = jnp.sum(jnp.where(query_row, turned, 0.0), axis=0, keepdims=True)
         return one.astype(bf16).astype(f32)
 
-    query_g = query(query_g_ref, basis_g)
-    query_h = query(query_h_ref, basis_h)
+    query_g = query(query_rows_g, basis_g)
+    query_h = query(query_rows_h, basis_h)
+    for j in range(width_d // 128):
+        small[k, x, z, j : j + 1, :] = query_g[:, j * 128 : (j + 1) * 128]
+    for j in range(width_ff // 128):
+        small[k, x, z, 16 + j : 17 + j, :] = query_h[:, j * 128 : (j + 1) * 128]
+
+    def ask_near(half):
+        return pltpu.make_async_remote_copy(
+            small.at[k, x, half],
+            small.at[k, x, half],
+            ask_s.at[0],
+            ask_r.at[0],
+            device_id={"dp_1": 1 - z},
+            device_id_type=MESH,
+        )
+
+    def ask_line(d, line):
+        return pltpu.make_async_remote_copy(
+            small.at[k, line],
+            small.at[k, line],
+            ask_s.at[d],
+            ask_r.at[d],
+            device_id={"dp_0": lax.rem(x + d, 4)},
+            device_id_type=MESH,
+        )
+
+    def ask_core(side):
+        return pltpu.make_async_remote_copy(
+            small.at[side],
+            small.at[side],
+            ask_s.at[4],
+            ask_r.at[4],
+            device_id={"dp_2": 1 - k},
+            device_id_type=MESH,
+        )
+
+    ask_near(z).start()
     for first, last in ((1, experts // 2), (experts // 2, experts)):
         each(first, last, lambda d: dg_copy(d).wait_recv())
         row_g.append(
@@ -205,6 +265,12 @@
                 first * capacity,
             )
         )
+        if first == 1:
+            ask_near(1 - z).wait_recv()
+            each(1, 4, lambda d: ask_line(d, x).start())
+        else:
+            each(1, 4, lambda d: ask_line(d, lax.rem(x + 4 - d, 4)).wait_recv())
+            ask_core(k).start()
     each(1, experts, lambda d: dh_copy(d).wait_recv())
     row_h = rotate(
         jnp.concatenate(
@@ -271,8 +337,8 @@
 
     def small_copy(d, slot):
         return pltpu.make_async_remote_copy(
-            small.at[me],
-            small.at[slot],
+            sums.at[me],
+            sums.at[slot],
             small_s.at[d],
             small_r.at[d],
             device_id=dp_id(lax.rem(me + d, 2 * chips)),
@@ -295,11 +361,7 @@
 
     def share():
         own_sum = jnp.sum(jnp.concatenate(row_g, axis=0) * row_h, axis=0, keepdims=True)
-        for j in range(width_d // 128):
-            small[me, j : j + 1, :] = query_g[:, j * 128 : (j + 1) * 128]
-        for j in range(width_ff // 128):
-            small[me, 16 + j : 17 + j, :] = query_h[:, j * 128 : (j + 1) * 128]
-        small[me, 22:24, :] = jnp.broadcast_to(own_sum, (2, 128))
+        sums[me] = jnp.broadcast_to(own_sum, (8, 128))
         each(1, 2 * chips, lambda d: small_copy(d, me).start())
 
     def stage_one(c):
@@ -331,13 +393,12 @@
         def step(t, _):
             parts = []
             for j in range(group):
-                n = t * group + j
                 pieces = []
                 for q in range(2 * chips):
                     d = (q % chips) * 2 + q // chips
                     pieces.append(
                         g_ref[:, d * CHUNK : (d + 1) * CHUNK]
-                        * small[n, d : d + 1, :].astype(bf16)
+                        * small[j % 2, t, j // 2, d : d + 1, :].astype(bf16)
                     )
                 parts.append(jnp.concatenate(pieces, axis=1))
             scaled = jnp.concatenate(parts, axis=0)
@@ -355,7 +416,7 @@
                         j * rows : (j + 1) * rows, half * CHUNK : (half + 1) * CHUNK
                     ] * (
                         h_ref[:, c * CHUNK : (c + 1) * CHUNK].astype(f32)
-                        * small[n, 16 + c : 17 + c, :]
+                        * small[j % 2, t, j // 2, 16 + c : 17 + c, :]
                     )
                     value = term if value is None else value + term
                 total = total + jnp.where(
@@ -376,11 +437,12 @@
     stage_one(1)
     spread(2)
     each(1, 2 * chips, small_arrival)
-    complete = small[0, 22:23, :]
+    complete = sums[0, 0:1, :]
     for n in range(1, 2 * chips):
-        complete = complete + small[n, 22:23, :]
+        complete = complete + sums[n, 0:1, :]
     level = damp_ref[0] * (complete * (scale / (width_d * width_ff)) + eps)
 
+    ask_core(1 - k).wait_recv()
     stages = {"A": stage_one, "C": lambda c: stage_two(c, level), "E": stage_three, "R": ready}
     for act, c, *span in ORDER:
         if act == "S":
@@ -388,7 +450,12 @@
         else:
             stages[act](c)
 
-    ret_out[...] = (acc[...] / root).reshape(ret_out.shape)
+    turned_scores = (acc[...] / root).T[: ret_out.shape[1], :]
+    blank = jnp.zeros((ret_out.shape[1], 128 - capacity), f32)
+    for d in range(experts):
+        ret_out[d] = jnp.concatenate(
+            [turned_scores[:, d * capacity : (d + 1) * capacity], blank], axis=1
+        )
 
     def ret_copy(d, slot):
         return pltpu.make_async_remote_copy(
@@ -402,24 +469,37 @@
 
     each(1, experts, lambda d: ret_copy(d, e).start())
     ret_in[e] = ret_out[0]
-    each(1, experts, lambda d: ret_copy(d, lax.rem(e + d, experts)).wait_recv())
-    result = lax.dot_general(
-        ret_in[...].reshape(experts * capacity, -1),
-        chosen,
-        (((0,), (0,)), ((), ())),
-        preferred_element_type=f32,
-        precision=lax.Precision.HIGHEST,
-    )
-    for j in range(top):
-        out_ref[j] = result[: out_ref.shape[1], j * tokens : (j + 1) * tokens]
     for c in range(chunks):
         each(1, chips, lambda d: rs_copy(c, d).wait_send())
         each(1, chips, lambda d: ag_copy(c, d).wait_send())
         cg_copy(c, k).wait_send()
     each(1, 2 * chips, lambda d: small_copy(d, me).wait_send())
-    each(1, experts, lambda d: ret_copy(d, e).wait_send())
+    ask_near(z).wait_send()
+    each(1, 4, lambda d: ask_line(d, x).wait_send())
+    ask_core(k).wait_send()
     each(1, experts, lambda d: dg_copy(d).wait_send())
     each(1, experts, lambda d: dh_copy(d).wait_send())
+    each(1, experts, lambda d: ret_copy(d, lax.rem(e + d, experts)).wait_recv())
+    arrived = jnp.concatenate([ret_in[j] for j in range(experts)], axis=1)
+    high = arrived.astype(bf16)
+    rest = arrived - high.astype(f32)
+    middle = rest.astype(bf16)
+    low = (rest - middle.astype(f32)).astype(bf16)
+    result = jnp.dot(
+        jnp.concatenate([high, middle, low], axis=0),
+        back[...].reshape(experts * 128, sent),
+        preferred_element_type=f32,
+    )
+    queries = ret_out.shape[1]
+    result = result[:queries] + result[queries : 2 * queries] + result[2 * queries :]
+    for j in range(top):
+        out_ref[j] = result[:, j * tokens : (j + 1) * tokens]
+    each(1, experts, lambda d: ret_copy(d, e).wait_send())
+
+
+def write_kernel(picked_ref, sums_ref, scores_ref, corr_ref):
+    scores_ref[...] = picked_ref[...]
+    corr_ref[...] = sums_ref[...]
 
 
 def body(
@@ -456,11 +536,15 @@
             jax.ShapeDtypeStruct((top, replicas, tokens), f32),
             jax.ShapeDtypeStruct((block, width_ff), f32),
         ),
-        in_specs=[vmem] * 4 + [anywhere] * 2 + [vmem] * 2 + [smem] * 2,
+        in_specs=[vmem] * 2 + [anywhere] * 6 + [smem] * 2,
         out_specs=(vmem, vmem),
         scratch_shapes=[
             pltpu.VMEM((width_d, width_d), bf16),
             pltpu.VMEM((width_ff, width_ff), bf16),
+            pltpu.VMEM(token_hidden.shape, bf16),
+            pltpu.VMEM(token_grad.shape, bf16),
+            pltpu.VMEM(query_grad.shape[1:], bf16),
+            pltpu.VMEM(query_hidden.shape[1:], bf16),
             pltpu.VMEM((experts, capacity, width_d), bf16),
             pltpu.VMEM((experts, capacity, width_ff), bf16),
             pltpu.VMEM((experts, capacity, width_d), bf16),
@@ -469,22 +553,26 @@
             pltpu.VMEM((rows, width_ff), bf16),
             pltpu.VMEM((rows, width_d), bf16),
             pltpu.VMEM((rows, width_ff), bf16),
-            pltpu.VMEM((replicas, 24, 128), f32),
+            pltpu.VMEM((2, chips // 2, 2, 24, 128), f32),
+            pltpu.VMEM((replicas, 8, 128), f32),
+            pltpu.VMEM((experts, 128, tokens * top), bf16),
             pltpu.VMEM((chunks, 2, chips, CHUNK, block), bf16),
             pltpu.VMEM((chunks, chips, CHUNK, block), bf16),
             pltpu.VMEM((chunks, chips, CHUNK, block), bf16),
             pltpu.VMEM((chunks, chips, CHUNK, block), bf16),
             pltpu.VMEM((chunks, 2, chips, block, CHUNK), bf16),
             pltpu.VMEM((rows, 128), f32),
-            pltpu.VMEM((experts, capacity, 128), f32),
-            pltpu.VMEM((experts, capacity, 128), f32),
-            dma((2,)),
+            pltpu.VMEM((experts, replicas, 128), f32),
+            pltpu.VMEM((experts, replicas, 128), f32),
+            dma((6,)),
             dma((experts,)),
             dma((experts,)),
             dma((experts,)),
             dma((experts,)),
             dma((replicas,)),
             dma((replicas,)),
+            dma((5,)),
+            dma((5,)),
             dma((chunks,)),
             dma((chunks,)),
             dma((chunks, chips)),
@@ -511,6 +599,13 @@
         query_ids,
         damping,
     )
+    picked, corrections = pl.pallas_call(
+        write_kernel,
+        out_shape=tuple(jax.ShapeDtypeStruct(a.shape, f32) for a in (picked, corrections)),
+        in_specs=[vmem] * 2,
+        out_specs=(vmem, vmem),
+        compiler_params=pltpu.CompilerParams(vmem_limit_bytes=2 * 1024 * 1024),
+    )(picked, corrections)
     return (picked.transpose(2, 0, 1), corrections[None])
 
 

time: 111 us -> 107 us (0.964)
  Pallas kernels: 104 us -> 102 us
  local copies, waits for them, and re-layouts: 3.09 us -> 1.71 us
    pallas_call x1, Pallas kernels: 104 us -> 101 us  [body(): pl.pallas_call(functools.partial(back_kernel, 1.0 / (replicas * experts *...]
    unnamed x2 -> x4, local copies, waits for them, and re-layouts: 3.09 us -> 1.71 us
where the time goes in v5:
time: 107 us; the launch traced here: 105 us
  Pallas kernels  102 us (95%)
  between operations  1.94 us (2%)
  local copies, waits for them, and re-layouts  1.71 us (2%)
    pallas_call x1, Pallas kernels, body(): pl.pallas_call(functools.partial(back_kernel, 1.0 / (replicas * experts *...  101 us

profile of v5, /device:TPU:0, one launch (start us, length us, event | category | flops | bytes accessed | tf_op | source)
XLA Modules:
  0.0 105.4 jit_solution(4915778120167731829)
XLA Ops:
  1.9 101.0 %shard_map.113 = (f32[2,16,128]{2,1,0:T(8,128)}, f32[128,768]{1,0:T(8,128)}) custom-call(s32[2,128]{1,0:T(2,128)} %bitcast.12, f32[2,128]{1,0:T(2,128)} %bitcast.13, bf16[128,2,768]{2,1,0:T(2,128)(2,1)} %hidden_ref.1, bf16[128,2048]{1,0:T(8,128)(2,1)} %grad_ref.1, bf16[2048,2048]{1,0:T(8,128)(2,1)} %bitcast.8, bf16[768,768]{1,0:T(8,128)(2,1)} %bitcast.9, ...), custom_call_target="tpu_custom_call" | custom-call | tf_op jit(solution)/shard_map/pallas_call | solution.py:531
  102.9 0.0 copy-start
  102.9 1.0 copy-done
  103.9 0.0 copy-start.1
  103.9 0.7 copy-done.1
  104.6 0.8 shard_map.114
Async XLA Ops:
  102.9 1.0 copy-start
  103.9 0.7 copy-start.1

commit v6 on v5

--- a/solution.py
+++ b/solution.py
@@ -18,10 +18,10 @@
 MESH = pl.DeviceIdType.MESH
 CHUNK = 128
 ORDER = (
-    ("C", 0), ("A", 2), ("C", 1), ("A", 3), ("E", 0), ("C", 2), ("A", 4), ("E", 1), ("R", 0),
-    ("R", 1), ("S", 0, 0, 1), ("C", 3), ("A", 5), ("S", 0, 1, 2), ("E", 2), ("S", 0, 2, 4),
-    ("C", 4), ("E", 3), ("R", 2), ("R", 3), ("S", 1, 0, 1), ("C", 5), ("S", 1, 1, 3), ("E", 4),
-    ("S", 1, 3, 4), ("E", 5), ("R", 4), ("R", 5), ("S", 2, 0, 4),
+    ("C", 0), ("C", 1), ("A", 2), ("A", 3), ("E", 0), ("E", 1), ("R", 0), ("R", 1), ("S", 0, 0, 1),
+    ("C", 2), ("S", 0, 1, 2), ("C", 3), ("A", 4), ("S", 0, 2, 4), ("E", 2), ("A", 5), ("E", 3),
+    ("R", 2), ("R", 3), ("S", 1, 0, 1), ("C", 4), ("S", 1, 1, 2), ("C", 5), ("S", 1, 2, 4),
+    ("E", 4), ("E", 5), ("R", 4), ("R", 5), ("S", 2, 0, 4),
 )
 
 
@@ -56,6 +56,7 @@
     hsq,
     small,
     sums,
+    corr,
     back,
     part,
     nearby,
@@ -375,7 +376,7 @@
         for d in range(1, chips):
             total = total + far[c, d].astype(f32)
         block = total.T * scale
-        corr_ref[:, c * CHUNK : (c + 1) * CHUNK] = block
+        corr[:, c * CHUNK : (c + 1) * CHUNK] = block
         inv[c, k, xz] = (1.0 / (block + level)).astype(bf16)
         each(1, chips, lambda d: ag_copy(c, d).start())
 
@@ -425,7 +426,7 @@
             acc[...] = total
             return 0
 
-        lax.fori_loop(first, last, step, 0)
+        lax.fori_loop(first + z // 2, last + z // 2, step, 0)
 
     def small_arrival(d):
         small_copy(d, lax.rem(me + 2 * chips - d, 2 * chips)).wait_recv()
@@ -468,6 +469,8 @@
         )
 
     each(1, experts, lambda d: ret_copy(d, e).start())
+    leave = pltpu.make_async_copy(corr, corr_ref, basis_sem.at[6])
+    leave.start()
     ret_in[e] = ret_out[0]
     for c in range(chunks):
         each(1, chips, lambda d: rs_copy(c, d).wait_send())
@@ -495,11 +498,26 @@
     for j in range(top):
         out_ref[j] = result[:, j * tokens : (j + 1) * tokens]
     each(1, experts, lambda d: ret_copy(d, e).wait_send())
-
-
-def write_kernel(picked_ref, sums_ref, scores_ref, corr_ref):
-    scores_ref[...] = picked_ref[...]
-    corr_ref[...] = sums_ref[...]
+    leave.wait()
+
+
+def write_kernel(picked_ref, sums_ref, scores_ref, corr_ref, picked, sums, sems):
+    pairs = ((sums_ref, sums, corr_ref), (picked_ref, picked, scores_ref))
+    taken = [
+        pltpu.make_async_copy(source, held, sems.at[0, i])
+        for i, (source, held, _) in enumerate(pairs)
+    ]
+    put = [
+        pltpu.make_async_copy(held, target, sems.at[1, i])
+        for i, (_, held, target) in enumerate(pairs)
+    ]
+    for copy in taken:
+        copy.start()
+    for first, second in zip(taken, put):
+        first.wait()
+        second.start()
+    for copy in put:
+        copy.wait()
 
 
 def body(
@@ -537,7 +555,7 @@
             jax.ShapeDtypeStruct((block, width_ff), f32),
         ),
         in_specs=[vmem] * 2 + [anywhere] * 6 + [smem] * 2,
-        out_specs=(vmem, vmem),
+        out_specs=(vmem, anywhere),
         scratch_shapes=[
             pltpu.VMEM((width_d, width_d), bf16),
             pltpu.VMEM((width_ff, width_ff), bf16),
@@ -555,6 +573,7 @@
             pltpu.VMEM((rows, width_ff), bf16),
             pltpu.VMEM((2, chips // 2, 2, 24, 128), f32),
             pltpu.VMEM((replicas, 8, 128), f32),
+            pltpu.VMEM((block, width_ff), f32),
             pltpu.VMEM((experts, 128, tokens * top), bf16),
             pltpu.VMEM((chunks, 2, chips, CHUNK, block), bf16),
             pltpu.VMEM((chunks, chips, CHUNK, block), bf16),
@@ -564,7 +583,7 @@
             pltpu.VMEM((rows, 128), f32),
             pltpu.VMEM((experts, replicas, 128), f32),
             pltpu.VMEM((experts, replicas, 128), f32),
-            dma((6,)),
+            dma((7,)),
             dma((experts,)),
             dma((experts,)),
             dma((experts,)),
@@ -602,9 +621,14 @@
     picked, corrections = pl.pallas_call(
         write_kernel,
         out_shape=tuple(jax.ShapeDtypeStruct(a.shape, f32) for a in (picked, corrections)),
-        in_specs=[vmem] * 2,
-        out_specs=(vmem, vmem),
-        compiler_params=pltpu.CompilerParams(vmem_limit_bytes=2 * 1024 * 1024),
+        in_specs=[anywhere] * 2,
+        out_specs=(anywhere, anywhere),
+        scratch_shapes=[
+            pltpu.VMEM(picked.shape, f32),
+            pltpu.VMEM(corrections.shape, f32),
+            dma((2, 2)),
+        ],
+        compiler_params=pltpu.CompilerParams(vmem_limit_bytes=60 * 1024 * 1024),
     )(picked, corrections)
     return (picked.transpose(2, 0, 1), corrections[None])
 

time: 107 us -> 105 us (0.981); the launches traced: 105 us -> 105 us
  local copies, waits for them, and re-layouts: 1.71 us -> 0 us
    unnamed x4 -> x0, local copies, waits for them, and re-layouts: 1.71 us -> none
where the time goes in v6:
time: 105 us
  Pallas kernels  103 us (98%)
  between operations  2.11 us (2%)
    pallas_call x1, Pallas kernels, body(): pl.pallas_call(functools.partial(back_kernel, 1.0 / (replicas * experts *...  101 us

profile of v6, /device:TPU:0, one launch (start us, length us, event | category | flops | bytes accessed | tf_op | source)
XLA Modules:
  0.0 104.8 jit_solution(13340942487254476015)
XLA Ops:
  1.9 100.9 %shard_map.113 = (f32[2,16,128]{2,1,0:T(8,128)}, f32[128,768]{1,0:T(8,128)}) custom-call(s32[2,128]{1,0:T(2,128)} %bitcast.12, f32[2,128]{1,0:T(2,128)} %bitcast.13, bf16[128,2,768]{2,1,0:T(2,128)(2,1)} %hidden_ref.1, bf16[128,2048]{1,0:T(8,128)(2,1)} %grad_ref.1, bf16[2048,2048]{1,0:T(8,128)(2,1)} %bitcast.8, bf16[768,768]{1,0:T(8,128)(2,1)} %bitcast.9, ...), custom_call_target="tpu_custom_call" | custom-call | tf_op jit(solution)/shard_map/pallas_call | solution.py:549
  102.8 1.8 %shard_map.114 = (f32[2,16,128]{2,1,0:T(8,128)}, f32[128,768]{1,0:T(8,128)}) custom-call(f32[2,16,128]{2,1,0:T(8,128)} %get-tuple-element.6.picked_ref, f32[128,768]{1,0:T(8,128)} %get-tuple-element.7.sums_ref), custom_call_target="tpu_custom_call" | custom-call | tf_op jit(solution)/shard_map/pallas_call | solution.py:621

commit v7 on v6

--- a/solution.py
+++ b/solution.py
@@ -16,13 +16,18 @@
 
 
 MESH = pl.DeviceIdType.MESH
-CHUNK = 128
+WIDE = 256
 ORDER = (
-    ("C", 0), ("C", 1), ("A", 2), ("A", 3), ("E", 0), ("E", 1), ("R", 0), ("R", 1), ("S", 0, 0, 1),
-    ("C", 2), ("S", 0, 1, 2), ("C", 3), ("A", 4), ("S", 0, 2, 4), ("E", 2), ("A", 5), ("E", 3),
-    ("R", 2), ("R", 3), ("S", 1, 0, 1), ("C", 4), ("S", 1, 1, 2), ("C", 5), ("S", 1, 2, 4),
-    ("E", 4), ("E", 5), ("R", 4), ("R", 5), ("S", 2, 0, 4),
+    ("C", 0), ("A", 2), ("C", 1), ("A", 3), ("E", 0), ("R", 0), ("S", 0, 0, 2), ("C", 2), ("A", 4),
+    ("S", 0, 2, 3), ("E", 1), ("S", 0, 3, 4), ("R", 1), ("S", 1, 0, 2), ("C", 3), ("A", 5),
+    ("S", 1, 2, 3), ("E", 2), ("S", 1, 3, 4), ("R", 2), ("S", 2, 0, 2), ("C", 4), ("S", 2, 2, 3),
+    ("E", 3), ("S", 2, 3, 4), ("R", 3), ("S", 3, 0, 2), ("C", 5), ("S", 3, 2, 3), ("E", 4),
+    ("S", 3, 3, 4), ("R", 4), ("S", 4, 0, 2), ("E", 5), ("S", 4, 2, 4), ("R", 5), ("S", 5, 0, 4),
 )
+
+
+def pair_of(tile, chips):
+    return tuple((q % chips) * 2 + q // chips for q in (2 * tile, 2 * tile + 1))
 
 
 def back_kernel(
@@ -57,6 +62,7 @@
     small,
     sums,
     corr,
+    ordered,
     back,
     part,
     nearby,
@@ -96,8 +102,18 @@
     capacity = held_g.shape[1]
     rows, width_d = g_ref.shape
     width_ff = h_ref.shape[1]
-    chunks = width_ff // CHUNK
+    chunks = part.shape[0]
+    half_rows = part.shape[3]
     bf16, f32 = jnp.bfloat16, jnp.float32
+
+    def halves(row, unit_half, tile):
+        return jnp.concatenate(
+            [
+                row[:, d * 128 + unit_half * half_rows : d * 128 + (unit_half + 1) * half_rows]
+                for d in pair_of(tile, chips)
+            ],
+            axis=1,
+        )
 
     def dp_id(index):
         return {"dp_0": index // 4, "dp_1": lax.rem(index // 2, 2), "dp_2": lax.rem(index, 2)}
@@ -220,7 +236,7 @@
     query_g = query(query_rows_g, basis_g)
     query_h = query(query_rows_h, basis_h)
     for j in range(width_d // 128):
-        small[k, x, z, j : j + 1, :] = query_g[:, j * 128 : (j + 1) * 128]
+        small[k, x, z, j : j + 1, :] = halves(query_g, j // chips, j % chips)
     for j in range(width_ff // 128):
         small[k, x, z, 16 + j : 17 + j, :] = query_h[:, j * 128 : (j + 1) * 128]
 
@@ -348,16 +364,15 @@
 
     def spread(pair):
         both = lax.dot_general(
-            hsq[:, pair * 2 * CHUNK : (pair + 1) * 2 * CHUNK],
             gsq[...],
+            hsq[:, pair * WIDE : (pair + 1) * WIDE],
             (((0,), (0,)), ((), ())),
             preferred_element_type=f32,
         ).astype(bf16)
         for half in range(2):
             for q in range(2 * chips):
-                part[2 * pair + half, q % 2, q // 2] = both[
-                    half * CHUNK : (half + 1) * CHUNK, q * CHUNK : (q + 1) * CHUNK
-                ]
+                first = q * 128 + half * half_rows
+                part[2 * pair + half, q % 2, q // 2] = both[first : first + half_rows, :]
             core_copy(2 * pair + half).start()
 
     def share():
@@ -375,8 +390,9 @@
         total = summed[c, xz].astype(f32)
         for d in range(1, chips):
             total = total + far[c, d].astype(f32)
-        block = total.T * scale
-        corr[:, c * CHUNK : (c + 1) * CHUNK] = block
+        block = total * scale
+        first, left = (c % 2) * half_rows, (c // 2) * WIDE
+        corr[first : first + half_rows, left : left + WIDE] = block
         inv[c, k, xz] = (1.0 / (block + level)).astype(bf16)
         each(1, chips, lambda d: ag_copy(c, d).start())
 
@@ -390,33 +406,33 @@
     lane = lax.broadcasted_iota(jnp.int32, acc.shape, 1)
     group = 4
 
-    def score(pair, first, last):
+    def score(unit, first, last):
+        left = (unit // 2) * WIDE
+
         def step(t, _):
             parts = []
             for j in range(group):
                 pieces = []
-                for q in range(2 * chips):
-                    d = (q % chips) * 2 + q // chips
+                for tile in range(chips):
+                    row = (unit % 2) * chips + tile
                     pieces.append(
-                        g_ref[:, d * CHUNK : (d + 1) * CHUNK]
-                        * small[j % 2, t, j // 2, d : d + 1, :].astype(bf16)
+                        ordered[unit % 2, :, tile * 128 : (tile + 1) * 128]
+                        * small[j % 2, t, j // 2, row : row + 1, :].astype(bf16)
                     )
                 parts.append(jnp.concatenate(pieces, axis=1))
             scaled = jnp.concatenate(parts, axis=0)
-            weights = jnp.concatenate(
-                [inv[2 * pair + half].reshape(width_d, CHUNK) for half in range(2)], axis=1
-            )
+            weights = inv[unit].reshape(width_d // 2, WIDE)
             product = jnp.dot(scaled, weights, preferred_element_type=f32)
             total = acc[...]
             for j in range(group):
                 n = t * group + j
                 value = None
-                for half in range(2):
-                    c = 2 * pair + half
+                for side in range(WIDE // 128):
+                    c = left // 128 + side
                     term = product[
-                        j * rows : (j + 1) * rows, half * CHUNK : (half + 1) * CHUNK
+                        j * rows : (j + 1) * rows, side * 128 : (side + 1) * 128
                     ] * (
-                        h_ref[:, c * CHUNK : (c + 1) * CHUNK].astype(f32)
+                        h_ref[:, c * 128 : (c + 1) * 128].astype(f32)
                         * small[j % 2, t, j // 2, 16 + c : 17 + c, :]
                     )
                     value = term if value is None else value + term
@@ -437,11 +453,15 @@
     stage_one(0)
     stage_one(1)
     spread(2)
+    for half in range(2):
+        for tile in range(chips):
+            ordered[half, :, tile * 128 : (tile + 1) * 128] = halves(g_ref, half, tile)
     each(1, 2 * chips, small_arrival)
     complete = sums[0, 0:1, :]
     for n in range(1, 2 * chips):
         complete = complete + sums[n, 0:1, :]
     level = damp_ref[0] * (complete * (scale / (width_d * width_ff)) + eps)
+    level = jnp.concatenate([level] * (WIDE // 128), axis=1)
 
     ask_core(1 - k).wait_recv()
     stages = {"A": stage_one, "C": lambda c: stage_two(c, level), "E": stage_three, "R": ready}
@@ -539,7 +559,7 @@
     capacity = tokens * top * 3 // (2 * experts)
     rows = experts * capacity
     chips = replicas // 2
-    chunks = width_ff // CHUNK
+    chunks = 2 * width_ff // WIDE
     bf16, f32 = jnp.bfloat16, jnp.float32
     block = width_d // replicas
     dma = pltpu.SemaphoreType.DMA
@@ -574,12 +594,13 @@
             pltpu.VMEM((2, chips // 2, 2, 24, 128), f32),
             pltpu.VMEM((replicas, 8, 128), f32),
             pltpu.VMEM((block, width_ff), f32),
+            pltpu.VMEM((2, rows, width_d // 2), bf16),
             pltpu.VMEM((experts, 128, tokens * top), bf16),
-            pltpu.VMEM((chunks, 2, chips, CHUNK, block), bf16),
-            pltpu.VMEM((chunks, chips, CHUNK, block), bf16),
-            pltpu.VMEM((chunks, chips, CHUNK, block), bf16),
-            pltpu.VMEM((chunks, chips, CHUNK, block), bf16),
-            pltpu.VMEM((chunks, 2, chips, block, CHUNK), bf16),
+            pltpu.VMEM((chunks, 2, chips, block // 2, WIDE), bf16),
+            pltpu.VMEM((chunks, chips, block // 2, WIDE), bf16),
+            pltpu.VMEM((chunks, chips, block // 2, WIDE), bf16),
+            pltpu.VMEM((chunks, chips, block // 2, WIDE), bf16),
+            pltpu.VMEM((chunks, 2, chips, block // 2, WIDE), bf16),
             pltpu.VMEM((rows, 128), f32),
             pltpu.VMEM((experts, replicas, 128), f32),
             pltpu.VMEM((experts, replicas, 128), f32),

time: 105 us -> 101 us (0.962)
  Pallas kernels: 103 us -> 98.7 us
    pallas_call x1, Pallas kernels: 101 us -> 96.9 us  [body(): pl.pallas_call(functools.partial(back_kernel, 1.0 / (replicas * experts *...]
where the time goes in v7:
time: 101 us
  Pallas kernels  98.7 us (98%)
  between operations  2.11 us (2%)
    pallas_call x1, Pallas kernels, body(): pl.pallas_call(functools.partial(back_kernel, 1.0 / (replicas * experts *...  96.9 us

profile of v7, /device:TPU:0, one launch (start us, length us, event | category | flops | bytes accessed | tf_op | source)
XLA Modules:
  0.0 100.8 jit_solution(5140785189696172585)
XLA Ops:
  1.9 96.9 %shard_map.113 = (f32[2,16,128]{2,1,0:T(8,128)}, f32[128,768]{1,0:T(8,128)}) custom-call(s32[2,128]{1,0:T(2,128)} %bitcast.12, f32[2,128]{1,0:T(2,128)} %bitcast.13, bf16[128,2,768]{2,1,0:T(2,128)(2,1)} %hidden_ref.1, bf16[128,2048]{1,0:T(8,128)(2,1)} %grad_ref.1, bf16[2048,2048]{1,0:T(8,128)(2,1)} %bitcast.8, bf16[768,768]{1,0:T(8,128)(2,1)} %bitcast.9, ...), custom_call_target="tpu_custom_call" | custom-call | tf_op jit(solution)/shard_map/pallas_call | solution.py:569
  98.8 1.8 %shard_map.114 = (f32[2,16,128]{2,1,0:T(8,128)}, f32[128,768]{1,0:T(8,128)}) custom-call(f32[2,16,128]{2,1,0:T(8,128)} %get-tuple-element.6.picked_ref, f32[128,768]{1,0:T(8,128)} %get-tuple-element.7.sums_ref), custom_call_target="tpu_custom_call" | custom-call | tf_op jit(solution)/shard_map/pallas_call | solution.py:642

commit v8 on v7

--- a/solution.py
+++ b/solution.py
@@ -289,15 +289,18 @@
             each(1, 4, lambda d: ask_line(d, lax.rem(x + 4 - d, 4)).wait_recv())
             ask_core(k).start()
     each(1, experts, lambda d: dh_copy(d).wait_recv())
-    row_h = rotate(
-        jnp.concatenate(
+
+    def rotate_hidden(left, right):
+        value = jnp.concatenate(
             [send_h[e], held_h[1:experts].reshape((experts - 1) * capacity, width_ff)], axis=0
-        ),
-        basis_h,
-        h_ref,
-        hsq,
-        0,
-    )
+        )
+        turned = jnp.dot(value, basis_h[:, left:right], preferred_element_type=f32).astype(bf16)
+        h_ref[:, left:right] = turned
+        square = jnp.square(turned.astype(f32)).astype(bf16)
+        hsq[:, left:right] = square
+        return jnp.sum(square.astype(f32), axis=1, keepdims=True)
+
+    row_h = [rotate_hidden(0, WIDE)]
 
     def core_copy(c):
         return pltpu.make_async_remote_copy(
@@ -376,7 +379,9 @@
             core_copy(2 * pair + half).start()
 
     def share():
-        own_sum = jnp.sum(jnp.concatenate(row_g, axis=0) * row_h, axis=0, keepdims=True)
+        own_sum = jnp.sum(
+            jnp.concatenate(row_g, axis=0) * (row_h[0] + row_h[1]), axis=0, keepdims=True
+        )
         sums[me] = jnp.broadcast_to(own_sum, (8, 128))
         each(1, 2 * chips, lambda d: small_copy(d, me).start())
 
@@ -448,10 +453,11 @@
         small_copy(d, lax.rem(me + 2 * chips - d, 2 * chips)).wait_recv()
 
     spread(0)
+    row_h.append(rotate_hidden(WIDE, width_ff))
     share()
-    spread(1)
     stage_one(0)
     stage_one(1)
+    spread(1)
     spread(2)
     for half in range(2):
         for tile in range(chips):
@@ -522,7 +528,11 @@
 
 
 def write_kernel(picked_ref, sums_ref, scores_ref, corr_ref, picked, sums, sems):
-    pairs = ((sums_ref, sums, corr_ref), (picked_ref, picked, scores_ref))
+    pieces = 4
+    tall = sums.shape[0] // pieces
+    cuts = [pl.ds(i * tall, tall) for i in range(pieces)]
+    pairs = [(sums_ref.at[cut], sums.at[cut], corr_ref.at[cut]) for cut in cuts]
+    pairs.append((picked_ref, picked, scores_ref))
     taken = [
         pltpu.make_async_copy(source, held, sems.at[0, i])
         for i, (source, held, _) in enumerate(pairs)
@@ -647,7 +657,7 @@
         scratch_shapes=[
             pltpu.VMEM(picked.shape, f32),
             pltpu.VMEM(corrections.shape, f32),
-            dma((2, 2)),
+            dma((2, 5)),
         ],
         compiler_params=pltpu.CompilerParams(vmem_limit_bytes=60 * 1024 * 1024),
     )(picked, corrections)

time: 101 us -> 101 us (level)
  no operation moved by 1% of the time
where the time goes in v8:
time: 101 us
  Pallas kernels  99.2 us (98%)
  between operations  2.11 us (2%)
    pallas_call x1, Pallas kernels, body(): pl.pallas_call(functools.partial(back_kernel, 1.0 / (replicas * experts *...  97.4 us

profile of v8, /device:TPU:0, one launch (start us, length us, event | category | flops | bytes accessed | tf_op | source)
XLA Modules:
  0.0 101.3 jit_solution(5504484374548094984)
XLA Ops:
  1.9 97.4 %shard_map.113 = (f32[2,16,128]{2,1,0:T(8,128)}, f32[128,768]{1,0:T(8,128)}) custom-call(s32[2,128]{1,0:T(2,128)} %bitcast.12, f32[2,128]{1,0:T(2,128)} %bitcast.13, bf16[128,2,768]{2,1,0:T(2,128)(2,1)} %hidden_ref.1, bf16[128,2048]{1,0:T(8,128)(2,1)} %grad_ref.1, bf16[2048,2048]{1,0:T(8,128)(2,1)} %bitcast.8, bf16[768,768]{1,0:T(8,128)(2,1)} %bitcast.9, ...), custom_call_target="tpu_custom_call" | custom-call | tf_op jit(solution)/shard_map/pallas_call | solution.py:579
  99.3 1.8 %shard_map.114 = (f32[2,16,128]{2,1,0:T(8,128)}, f32[128,768]{1,0:T(8,128)}) custom-call(f32[2,16,128]{2,1,0:T(8,128)} %get-tuple-element.6.picked_ref, f32[128,768]{1,0:T(8,128)} %get-tuple-element.7.sums_ref), custom_call_target="tpu_custom_call" | custom-call | tf_op jit(solution)/shard_map/pallas_call | solution.py:652

commit v9 on v7

--- a/solution.py
+++ b/solution.py
@@ -18,10 +18,10 @@
 MESH = pl.DeviceIdType.MESH
 WIDE = 256
 ORDER = (
-    ("C", 0), ("A", 2), ("C", 1), ("A", 3), ("E", 0), ("R", 0), ("S", 0, 0, 2), ("C", 2), ("A", 4),
-    ("S", 0, 2, 3), ("E", 1), ("S", 0, 3, 4), ("R", 1), ("S", 1, 0, 2), ("C", 3), ("A", 5),
-    ("S", 1, 2, 3), ("E", 2), ("S", 1, 3, 4), ("R", 2), ("S", 2, 0, 2), ("C", 4), ("S", 2, 2, 3),
-    ("E", 3), ("S", 2, 3, 4), ("R", 3), ("S", 3, 0, 2), ("C", 5), ("S", 3, 2, 3), ("E", 4),
+    ("C", 0), ("A", 2), ("C", 1), ("A", 3), ("E", 0), ("R", 0), ("S", 0, 0, 1), ("C", 2), ("A", 4),
+    ("S", 0, 1, 3), ("E", 1), ("S", 0, 3, 4), ("R", 1), ("S", 1, 0, 1), ("C", 3), ("A", 5),
+    ("S", 1, 1, 3), ("E", 2), ("S", 1, 3, 4), ("R", 2), ("S", 2, 0, 1), ("C", 4), ("S", 2, 1, 3),
+    ("E", 3), ("S", 2, 3, 4), ("R", 3), ("S", 3, 0, 1), ("C", 5), ("S", 3, 1, 3), ("E", 4),
     ("S", 3, 3, 4), ("R", 4), ("S", 4, 0, 2), ("E", 5), ("S", 4, 2, 4), ("R", 5), ("S", 5, 0, 4),
 )
 

time: 101 us -> 100 us (0.990)
  no operation moved by 1% of the time
where the time goes in v9:
time: 100 us; the launch traced here: 99.9 us
  Pallas kernels  97.8 us (98%)
  between operations  2.11 us (2%)
    pallas_call x1, Pallas kernels, body(): pl.pallas_call(functools.partial(back_kernel, 1.0 / (replicas * experts *...  96.1 us

profile of v9, /device:TPU:0, one launch (start us, length us, event | category | flops | bytes accessed | tf_op | source)
XLA Modules:
  0.0 99.9 jit_solution(15769323631931118802)
XLA Ops:
  1.9 96.1 %shard_map.113 = (f32[2,16,128]{2,1,0:T(8,128)}, f32[128,768]{1,0:T(8,128)}) custom-call(s32[2,128]{1,0:T(2,128)} %bitcast.12, f32[2,128]{1,0:T(2,128)} %bitcast.13, bf16[128,2,768]{2,1,0:T(2,128)(2,1)} %hidden_ref.1, bf16[128,2048]{1,0:T(8,128)(2,1)} %grad_ref.1, bf16[2048,2048]{1,0:T(8,128)(2,1)} %bitcast.8, bf16[768,768]{1,0:T(8,128)(2,1)} %bitcast.9, ...), custom_call_target="tpu_custom_call" | custom-call | tf_op jit(solution)/shard_map/pallas_call | solution.py:569
  98.0 1.8 %shard_map.114 = (f32[2,16,128]{2,1,0:T(8,128)}, f32[128,768]{1,0:T(8,128)}) custom-call(f32[2,16,128]{2,1,0:T(8,128)} %get-tuple-element.6.picked_ref, f32[128,768]{1,0:T(8,128)} %get-tuple-element.7.sums_ref), custom_call_target="tpu_custom_call" | custom-call | tf_op jit(solution)/shard_map/pallas_call | solution.py:642
